TPU v7x, 512 devices: a whole 4x4x16 slice. The times are simulated.
512 devices in a mesh: seq: 64 (over x, z), head: 8 (over y, core).
Axes of the slice: x: 4, y: 4, z: 16, core: 2. Of those that a mesh axis runs over, the one named last changes fastest.
Arguments:
- queries: bfloat16 [16384, 8192], P('seq', 'head'), may hold values from -5 to 5
- key_rows: bfloat16 [16384, 8192], P('seq', 'head'), may hold values from -5 to 5
- values: bfloat16 [16384, 8192], P('seq', 'head'), may hold values from -6 to 6
- grad_out: bfloat16 [16384, 8192], P('seq', 'head'), may hold values from -6 to 6
- routes: int32 [64, 16384, 1], P('head', 'seq'), may hold values from 0 to 63; in each aligned block of 256 rows (0 to 255, 256 to 511, ..., all dimensions but the last counted through in order) at most 6 rows name the same one
Outputs:
- attended: bfloat16 [16384, 8192], P('seq', 'head')
- grad_query: bfloat16 [16384, 8192], P('seq', 'head')
- grad_key: bfloat16 [16384, 8192], P('seq', 'head')
- grad_value: bfloat16 [16384, 8192], P('seq', 'head')
Inputs may be any that keep to these rules, and one draw needn't show every extreme that they name: `routes`: for each head, no cluster is named by more than 6 of the 256 tokens of one index of seq, a bound that some block reaches of them.
All inputs are finite; a program needn't handle non-finite values.
Results may differ from a plain program's by a relative error of at most 0.0029.
The roundings to bfloat16 on the way count: a program that leaves them out, or rounds other values in their place, can miss the bound.
Values may be sent and summed in bfloat16 or wider, within the bound.
No kernel may reach another device: no remote copies, remote signals or barrier semaphores. Data moves between devices by JAX's collectives and lax.ppermute only.
A program may use at most 64 MiB of HBM per device.

v0:
```python
import math

import jax
import jax.numpy as jnp
from jax import lax
from jax.sharding import PartitionSpec as P


def forward_head(members):
    query_block, key_block, value_block, live_keys = members
    scaling = 1.0 / math.sqrt(query_block.shape[1])
    scores = jnp.dot(query_block, key_block.T, preferred_element_type=jnp.float32) * scaling
    masked = jnp.where(live_keys[None, :], scores, -1e30)
    row_peak = jnp.max(masked, axis=1, keepdims=True)
    weights = jnp.exp(masked - row_peak)
    probability = weights / jnp.sum(weights, axis=1, keepdims=True)
    output = jnp.dot(
        probability.astype(jnp.bfloat16), value_block, preferred_element_type=jnp.float32
    ).astype(jnp.bfloat16)
    return (probability, output)


def backward_head(members):
    query_block, key_block, value_block, grad_block, probability, output = members
    scaling = 1.0 / math.sqrt(query_block.shape[1])
    probability_low = probability.astype(jnp.bfloat16)
    grad_probability = jnp.dot(grad_block, value_block.T, preferred_element_type=jnp.float32)
    delta_rows = jnp.sum(
        grad_block.astype(jnp.float32) * output.astype(jnp.float32), axis=1, keepdims=True
    )
    grad_scores = (probability * (grad_probability - delta_rows)).astype(jnp.bfloat16)
    grad_query = (
        jnp.dot(grad_scores, key_block, preferred_element_type=jnp.float32) * scaling
    ).astype(jnp.bfloat16)
    grad_key = (
        jnp.dot(grad_scores.T, query_block, preferred_element_type=jnp.float32) * scaling
    ).astype(jnp.bfloat16)
    grad_value = jnp.dot(probability_low.T, grad_block, preferred_element_type=jnp.float32).astype(
        jnp.bfloat16
    )
    return (grad_query, grad_key, grad_value)


def live_mask(query_rows, live_counts):
    slot_count = query_rows.shape[1] // live_counts.shape[1]
    within = jnp.arange(query_rows.shape[1], dtype=jnp.int32) % slot_count
    return jnp.repeat(live_counts, slot_count, axis=1) > within[None, :]


def cluster_work(query_rows, key_part, value_rows, grad_rows, live_counts):
    live = live_mask(query_rows, live_counts)
    probability, output = lax.map(forward_head, (query_rows, key_part, value_rows, live))
    gradients = lax.map(
        backward_head, (query_rows, key_part, value_rows, grad_rows, probability, output)
    )
    return (output,) + tuple(gradients)


def body(queries, key_rows, values, grad_out, routes):
    token_count, feature_count = queries.shape
    head_count = routes.shape[0]
    head_size = feature_count // head_count
    owners = lax.axis_size("seq")
    slot_count = 3 * token_count // (2 * owners)
    row_count = owners * slot_count
    clusters = routes[:, :, 0]
    onehot = (clusters[:, :, None] == jnp.arange(owners, dtype=jnp.int32)[None, None, :]).astype(
        jnp.float32
    )
    token_ids = jnp.arange(token_count, dtype=jnp.int32)
    earlier = (token_ids[:, None] > token_ids[None, :]).astype(jnp.float32)
    before = jnp.einsum("ij,hjc->hic", earlier, onehot, precision=lax.Precision.HIGHEST)
    ranking = jnp.sum(before * onehot, axis=2).astype(jnp.int32)
    counts = jnp.sum(onehot, axis=1).astype(jnp.int32)
    position = clusters * slot_count + ranking
    matches = position[:, :, None] == jnp.arange(row_count, dtype=jnp.int32)[None, None, :]
    filled = jnp.any(matches, axis=1)
    source_row = jnp.sum(jnp.where(matches, token_ids[None, :, None], 0), axis=1)

    def pack_rows(tensor):
        head_view = tensor.reshape(token_count, head_count, head_size).transpose(1, 0, 2)
        picked = jnp.take_along_axis(head_view, source_row[:, :, None], axis=1)
        return jnp.where(filled[:, :, None], picked, jnp.zeros_like(picked))

    def unpack_rows(tensor):
        picked = jnp.take_along_axis(tensor, position[:, :, None], axis=1)
        return picked.transpose(1, 0, 2).reshape(token_count, feature_count)

    packed_query = pack_rows(queries)
    packed_key = pack_rows(key_rows)
    packed_value = pack_rows(values)
    packed_grad = pack_rows(grad_out)
    received = (
        lax.all_to_all(packed_query, "seq", split_axis=1, concat_axis=1, tiled=True),
        lax.all_to_all(packed_key, "seq", split_axis=1, concat_axis=1, tiled=True),
        lax.all_to_all(packed_value, "seq", split_axis=1, concat_axis=1, tiled=True),
        lax.all_to_all(packed_grad, "seq", split_axis=1, concat_axis=1, tiled=True),
        lax.all_to_all(counts, "seq", split_axis=1, concat_axis=1, tiled=True),
    )
    results = cluster_work(received[0], received[1], received[2], received[3], received[4])
    output_back = lax.all_to_all(results[0], "seq", split_axis=1, concat_axis=1, tiled=True)
    grads_back = (
        lax.all_to_all(results[1], "seq", split_axis=1, concat_axis=1, tiled=True),
        lax.all_to_all(results[2], "seq", split_axis=1, concat_axis=1, tiled=True),
        lax.all_to_all(results[3], "seq", split_axis=1, concat_axis=1, tiled=True),
    )
    returned = (output_back,) + tuple(grads_back)
    return (
        unpack_rows(returned[0]),
        unpack_rows(returned[1]),
        unpack_rows(returned[2]),
        unpack_rows(returned[3]),
    )


def solution(mesh):
    in_specs = (
        P("seq", "head"),
        P("seq", "head"),
        P("seq", "head"),
        P("seq", "head"),
        P("head", "seq", None),
    )
    out_specs = (P("seq", "head"), P("seq", "head"), P("seq", "head"), P("seq", "head"))
    return jax.shard_map(body, mesh=mesh, in_specs=in_specs, out_specs=out_specs, check_vma=False)
```

profile of v0, /device:TPU:1, one launch (start us, length us, event | category | flops | bytes accessed | tf_op | source)
XLA Modules:
  0.0 589.6 jit_solution(12658312375142266919)
XLA Ops:
  2.2 19.2 %all-to-all-start = ((s32[8,64,1]{0,2,1:T(1,128)}), s32[8,64,1]{0,2,1:T(1,128)S(1)}, u32[]{:S(2)}, u32[]{:S(2)}) async-start(s32[8,64,1]{0,2,1:T(1,128)} %copy.147), calls=%async_computation | async-start | bytes 65536 | tf_op jit(solution)/shard_map/all_to_all | solution.py:98
  21.8 1.3 compare_and_fusion
  24.2 1.2 copy.151
  26.2 16.4 %gather_fusion = bf16[3072,128]{1,0:T(8,128)(2,1)S(1)} fusion(bf16[8,256,128]{2,1,0:T(8,128)(2,1)S(1)} %bitcast.172, s32[3072]{0:T(1024)S(1)} %reshape.129), kind=kCustom, calls=%fused_computation.clone | custom fusion | bytes 1597440 | tf_op jit(solution)/shard_map/jit(take_along_axis)/gather | solution.py:82
  42.7 16.4 %gather_fusion.1 = bf16[3072,128]{1,0:T(8,128)(2,1)S(1)} fusion(bf16[8,256,128]{2,1,0:T(8,128)(2,1)S(1)} %bitcast.173, s32[3072]{0:T(1024)S(1)} %reshape.129), kind=kCustom, calls=%fused_computation.2.clone | custom fusion | bytes 1597440 | tf_op jit(solution)/shard_map/jit(take_along_axis)/gather | solution.py:82
  59.6 16.4 %gather_fusion.2 = bf16[3072,128]{1,0:T(8,128)(2,1)S(1)} fusion(bf16[8,256,128]{2,1,0:T(8,128)(2,1)S(1)} %bitcast.175, s32[3072]{0:T(1024)S(1)} %reshape.129), kind=kCustom, calls=%fused_computation.3.clone | custom fusion | bytes 1597440 | tf_op jit(solution)/shard_map/jit(take_along_axis)/gather | solution.py:82
  76.0 1.2 copy.170
  77.5 30.4 %gather_fusion.4 = bf16[3072,128]{1,0:T(8,128)(2,1)} fusion(bf16[8,256,128]{2,1,0:T(8,128)(2,1)S(1)} %bitcast.174, s32[3072]{0:T(1024)S(1)} %reshape.129), kind=kCustom, calls=%fused_computation.4.clone | custom fusion | bytes 1597440 | tf_op jit(solution)/shard_map/jit(take_along_axis)/gather | solution.py:82
  108.3 11.0 %fusion.45 = (bf16[8,384,128]{2,0,1:T(8,128)(2,1)}, bf16[8,384,128]{2,0,1:T(8,128)(2,1)S(1)}, bf16[8,384,128]{2,0,1:T(8,128)(2,1)}, bf16[8,384,128]{2,0,1:T(8,128)(2,1)}) fusion(bf16[8,384,128]{2,1,0:T(8,128)(2,1)} %bitcast.179, pred[8,384]{0,1:T(8,128)(4,1)S(1)} %copy.150, pred[8,384]{0,1:T(8,128)(4,1)S(1)} %copy.149, ...), kind=kLoop, calls=%fused_computation.67 | loop fusion | flops 3145728 | bytes 6297600 | tf_op jit(solution)/shard_map/jit(_where)/select_n | solution.py:83
  119.3 53.3 %all_to_all.49 = bf16[8,384,128]{2,0,1:T(8,128)(2,1)S(1)} all-to-all(bf16[8,384,128]{2,0,1:T(8,128)(2,1)} %get-tuple-element.232), channel_id=1, replica_groups=mesh['seq'=64,'head'=8] {'seq'}, dimensions={1} | all-to-all | bytes 1572864 | tf_op jit(solution)/shard_map/all_to_all | solution.py:94
  172.7 49.4 %all_to_all.50 = bf16[8,384,128]{2,0,1:T(8,128)(2,1)} all-to-all(bf16[8,384,128]{2,0,1:T(8,128)(2,1)S(1)} %get-tuple-element.230), channel_id=1, replica_groups=mesh['seq'=64,'head'=8] {'seq'}, dimensions={1} | all-to-all | bytes 1572864 | tf_op jit(solution)/shard_map/all_to_all | solution.py:95
  222.0 10.3 %all-to-all-start.3 = ((bf16[8,384,128]{2,0,1:T(8,128)(2,1)}), bf16[8,384,128]{2,0,1:T(8,128)(2,1)S(1)}, u32[]{:S(2)}, u32[]{:S(2)}) async-start(bf16[8,384,128]{2,0,1:T(8,128)(2,1)} %get-tuple-element.231), calls=%async_computation.3 | async-start | bytes 1572864 | tf_op jit(solution)/shard_map/all_to_all | solution.py:96
  233.9 37.5 %all-to-all-done.3 = bf16[8,384,128]{2,0,1:T(8,128)(2,1)S(1)} async-done(((bf16[8,384,128]{2,0,1:T(8,128)(2,1)}), bf16[8,384,128]{2,0,1:T(8,128)(2,1)S(1)}, u32[]{:S(2)}, u32[]{:S(2)}) %all-to-all-start.3) | async-done | bytes 786464 | tf_op jit(solution)/shard_map/all_to_all | solution.py:96
  271.5 10.3 %all-to-all-start.5 = ((bf16[8,384,128]{2,0,1:T(8,128)(2,1)}), bf16[8,384,128]{2,0,1:T(8,128)(2,1)S(1)}, u32[]{:S(2)}, u32[]{:S(2)}) async-start(bf16[8,384,128]{2,0,1:T(8,128)(2,1)} %get-tuple-element.229), calls=%async_computation.5 | async-start | bytes 1572864 | tf_op jit(solution)/shard_map/all_to_all | solution.py:97
  282.0 20.6 %while.26 = (s32[]{:T(128)}, f32[8,384,384]{1,2,0:T(8,128)}, bf16[8,384,128]{2,1,0:T(8,128)(2,1)S(1)}, pred[8,384]{1,0:T(8,128)(4,1)S(1)}, bf16[8,384,128]{2,1,0...) while((s32[]{:T(128)}, f32[8,384,384]{1,2,0:T(8,128)}, ...), condition=%wide.region_7.9_spmd, body=%wide.region_4.8_spmd.sunk | while | flops 77020416 | bytes 3358041 | solution.py:52
  282.1 1.2 fusion.78
  284.6 1.2 fusion.78
  287.2 1.2 fusion.78
  289.8 1.2 fusion.78
  292.4 1.2 fusion.78
  295.0 1.2 fusion.78
  297.5 1.2 fusion.78
  300.1 1.2 fusion.78
  303.6 17.4 %all-to-all-done.5 = bf16[8,384,128]{2,0,1:T(8,128)(2,1)S(1)} async-done(((bf16[8,384,128]{2,0,1:T(8,128)(2,1)}), bf16[8,384,128]{2,0,1:T(8,128)(2,1)S(1)}, u32[]{:S(2)}, u32[]{:S(2)}) %all-to-all-start.5) | async-done | bytes 786464 | tf_op jit(solution)/shard_map/all_to_all | solution.py:97
  324.1 50.2 %while.27 = (s32[]{:T(128)}, bf16[8,384,128]{2,1,0:T(8,128)(2,1)}, bf16[8,384,128]{2,1,0:T(8,128)(2,1)}, bf16[8,384,128]{2,1,0:T(8,128)(2,1)}, f32[8,384,384]{1,...) while((s32[]{:T(128)}, bf16[8,384,128]{2,1,0:T(8,128)(2,1)}, ...), condition=%wide.region_10.13_spmd, body=%wide.region_8.12_spmd.sunk | while | flops 152026752 | bytes 5414517 | solution.py:53
  324.2 1.1 constant_dynamic-slice_fusion.2
  325.6 1.2 fusion.90
  327.6 1.8 fusion.91
  331.8 1.2 fusion.90
  333.9 1.8 fusion.91
  336.8 1.1 constant_dynamic-slice_fusion.2
  338.1 1.2 fusion.90
  340.2 1.8 fusion.91
  344.4 1.2 fusion.90
  346.5 1.8 fusion.91
  349.3 1.1 constant_dynamic-slice_fusion.2
  350.7 1.2 fusion.90
  352.8 1.8 fusion.91
  356.9 1.2 fusion.90
  359.0 1.8 fusion.91
  361.9 1.1 constant_dynamic-slice_fusion.2
  363.2 1.2 fusion.90
  365.3 1.8 fusion.91
  369.5 1.2 fusion.90
  371.6 1.8 fusion.91
  374.2 2.6 copy.181
  376.8 10.1 %all-to-all-start.6 = ((bf16[8,384,128]{2,0,1:T(8,128)(2,1)}), bf16[8,384,128]{2,0,1:T(8,128)(2,1)S(1)}, u32[]{:S(2)}, u32[]{:S(2)}) async-start(bf16[8,384,128]{2,0,1:T(8,128)(2,1)} %copy.181), calls=%async_computation.6 | async-start | bytes 1572864 | tf_op jit(solution)/shard_map/all_to_all | solution.py:103
  386.9 1.4 copy.184
  388.4 37.9 %all-to-all-done.6 = bf16[8,384,128]{2,0,1:T(8,128)(2,1)S(1)} async-done(((bf16[8,384,128]{2,0,1:T(8,128)(2,1)}), bf16[8,384,128]{2,0,1:T(8,128)(2,1)S(1)}, u32[]{:S(2)}, u32[]{:S(2)}) %all-to-all-start.6) | async-done | bytes 786464 | tf_op jit(solution)/shard_map/all_to_all | solution.py:103
  426.3 9.9 %all-to-all-start.7 = ((bf16[8,384,128]{2,0,1:T(8,128)(2,1)}), bf16[8,384,128]{2,0,1:T(8,128)(2,1)S(1)}, u32[]{:S(2)}, u32[]{:S(2)}) async-start(bf16[8,384,128]{2,0,1:T(8,128)(2,1)} %copy.184), calls=%async_computation.7 | async-start | bytes 1572864 | tf_op jit(solution)/shard_map/all_to_all | solution.py:104
  436.2 2.5 copy.187
  438.7 37.0 %all-to-all-done.7 = bf16[8,384,128]{2,0,1:T(8,128)(2,1)S(1)} async-done(((bf16[8,384,128]{2,0,1:T(8,128)(2,1)}), bf16[8,384,128]{2,0,1:T(8,128)(2,1)S(1)}, u32[]{:S(2)}, u32[]{:S(2)}) %all-to-all-start.7) | async-done | bytes 786464 | tf_op jit(solution)/shard_map/all_to_all | solution.py:104
  475.7 9.7 %all-to-all-start.8 = ((bf16[8,384,128]{2,0,1:T(8,128)(2,1)}), bf16[8,384,128]{2,0,1:T(8,128)(2,1)S(1)}, u32[]{:S(2)}, u32[]{:S(2)}) async-start(bf16[8,384,128]{2,0,1:T(8,128)(2,1)} %copy.187), calls=%async_computation.8 | async-start | bytes 1572864 | tf_op jit(solution)/shard_map/all_to_all | solution.py:105
  485.5 1.4 copy.166
  486.9 38.1 %all-to-all-done.8 = bf16[8,384,128]{2,0,1:T(8,128)(2,1)S(1)} async-done(((bf16[8,384,128]{2,0,1:T(8,128)(2,1)}), bf16[8,384,128]{2,0,1:T(8,128)(2,1)S(1)}, u32[]{:S(2)}, u32[]{:S(2)}) %all-to-all-start.8) | async-done | bytes 786464 | tf_op jit(solution)/shard_map/all_to_all | solution.py:105
  525.0 10.1 %all-to-all-start.4 = ((bf16[8,384,128]{2,0,1:T(8,128)(2,1)}), bf16[8,384,128]{2,0,1:T(8,128)(2,1)}, u32[]{:S(2)}, u32[]{:S(2)}) async-start(bf16[8,384,128]{2,0,1:T(8,128)(2,1)} %copy.166), calls=%async_computation.4 | async-start | bytes 1572864 | tf_op jit(solution)/shard_map/all_to_all | solution.py:101
  535.3 11.2 %gather_fusion.5 = bf16[2048,128]{1,0:T(8,128)(2,1)S(1)} fusion(bf16[8,384,128]{2,1,0:T(8,128)(2,1)S(1)} %copy.182, s32[2048]{0:T(1024)S(1)} %bitcast.168), kind=kCustom, calls=%fused_computation.5.clone | custom fusion | bytes 1064960 | tf_op jit(solution)/shard_map/jit(take_along_axis)/gather | solution.py:86
  546.6 11.2 %gather_fusion.6 = bf16[2048,128]{1,0:T(8,128)(2,1)S(1)} fusion(bf16[8,384,128]{2,1,0:T(8,128)(2,1)S(1)} %copy.185, s32[2048]{0:T(1024)S(1)} %bitcast.169), kind=kCustom, calls=%fused_computation.6.clone | custom fusion | bytes 1064960 | tf_op jit(solution)/shard_map/jit(take_along_axis)/gather | solution.py:86
  557.9 11.2 %gather_fusion.7 = bf16[2048,128]{1,0:T(8,128)(2,1)S(1)} fusion(bf16[8,384,128]{2,1,0:T(8,128)(2,1)S(1)} %copy.188, s32[2048]{0:T(1024)S(1)} %bitcast.170), kind=kCustom, calls=%fused_computation.7.clone | custom fusion | bytes 1064960 | tf_op jit(solution)/shard_map/jit(take_along_axis)/gather | solution.py:86
  569.0 5.4 all-to-all-done.4
  574.5 1.2 copy.167
  575.7 11.2 %gather_fusion.3 = bf16[2048,128]{1,0:T(8,128)(2,1)S(1)} fusion(bf16[8,384,128]{2,1,0:T(8,128)(2,1)S(1)} %copy.167, s32[2048]{0:T(1024)S(1)} %bitcast.171), kind=kCustom, calls=%fused_computation.1.clone | custom fusion | bytes 1064960 | tf_op jit(solution)/shard_map/jit(take_along_axis)/gather | solution.py:86
  587.3 1.1 copy_bitcast_fusion
  588.5 1.1 copy_bitcast_fusion.2
  (121 shorter events, 44.5 us)
Async XLA Ops:
  2.2 23.6 %copy-start.3 = (bf16[256,1024]{1,0:T(8,128)(2,1)S(1)}, bf16[256,1024]{1,0:T(8,128)(2,1)}, u32[]{:S(2)}) copy-start(bf16[256,1024]{1,0:T(8,128)(2,1)} %param.14) | copy-start | bytes 1572868
  2.2 117.1 %all-to-all-start = ((s32[8,64,1]{0,2,1:T(1,128)}), s32[8,64,1]{0,2,1:T(1,128)S(1)}, u32[]{:S(2)}, u32[]{:S(2)}) async-start(s32[8,64,1]{0,2,1:T(1,128)} %copy.147), calls=%async_computation | async-start | bytes 65536 | tf_op jit(solution)/shard_map/all_to_all | solution.py:98
  42.7 16.4 %copy-start.4 = (bf16[256,1024]{1,0:T(8,128)(2,1)S(1)}, bf16[256,1024]{1,0:T(8,128)(2,1)}, u32[]{:S(2)}) copy-start(bf16[256,1024]{1,0:T(8,128)(2,1)} %param.15) | copy-start | bytes 1572868
  222.0 10.9 %copy-start = (bf16[8,384,128]{2,0,1:T(8,128)(2,1)S(1)}, bf16[8,384,128]{2,0,1:T(8,128)(2,1)}, u32[]{:S(2)}) copy-start(bf16[8,384,128]{2,0,1:T(8,128)(2,1)} %all_to_all.50) | copy-start | bytes 2359300
  222.0 49.4 %all-to-all-start.3 = ((bf16[8,384,128]{2,0,1:T(8,128)(2,1)}), bf16[8,384,128]{2,0,1:T(8,128)(2,1)S(1)}, u32[]{:S(2)}, u32[]{:S(2)}) async-start(bf16[8,384,128]{2,0,1:T(8,128)(2,1)} %get-tuple-element.231), calls=%async_computation.3 | async-start | bytes 1572864 | tf_op jit(solution)/shard_map/all_to_all | solution.py:96
  271.5 49.5 %all-to-all-start.5 = ((bf16[8,384,128]{2,0,1:T(8,128)(2,1)}), bf16[8,384,128]{2,0,1:T(8,128)(2,1)S(1)}, u32[]{:S(2)}, u32[]{:S(2)}) async-start(bf16[8,384,128]{2,0,1:T(8,128)(2,1)} %get-tuple-element.229), calls=%async_computation.5 | async-start | bytes 1572864 | tf_op jit(solution)/shard_map/all_to_all | solution.py:97
  302.7 0.9 copy-start.2
  374.2 12.7 %copy-start.1 = (bf16[8,384,128]{2,1,0:T(8,128)(2,1)S(1)}, bf16[8,384,128]{2,1,0:T(8,128)(2,1)}, u32[]{:S(2)}) copy-start(bf16[8,384,128]{2,1,0:T(8,128)(2,1)} %get-tuple-element.101) | copy-start | bytes 2359300
  376.8 49.4 %all-to-all-start.6 = ((bf16[8,384,128]{2,0,1:T(8,128)(2,1)}), bf16[8,384,128]{2,0,1:T(8,128)(2,1)S(1)}, u32[]{:S(2)}, u32[]{:S(2)}) async-start(bf16[8,384,128]{2,0,1:T(8,128)(2,1)} %copy.181), calls=%async_computation.6 | async-start | bytes 1572864 | tf_op jit(solution)/shard_map/all_to_all | solution.py:103
  426.3 49.5 %all-to-all-start.7 = ((bf16[8,384,128]{2,0,1:T(8,128)(2,1)}), bf16[8,384,128]{2,0,1:T(8,128)(2,1)S(1)}, u32[]{:S(2)}, u32[]{:S(2)}) async-start(bf16[8,384,128]{2,0,1:T(8,128)(2,1)} %copy.184), calls=%async_computation.7 | async-start | bytes 1572864 | tf_op jit(solution)/shard_map/all_to_all | solution.py:104
  475.7 49.2 %all-to-all-start.8 = ((bf16[8,384,128]{2,0,1:T(8,128)(2,1)}), bf16[8,384,128]{2,0,1:T(8,128)(2,1)S(1)}, u32[]{:S(2)}, u32[]{:S(2)}) async-start(bf16[8,384,128]{2,0,1:T(8,128)(2,1)} %copy.187), calls=%async_computation.8 | async-start | bytes 1572864 | tf_op jit(solution)/shard_map/all_to_all | solution.py:105
  485.4 49.7 %copy-start.5 = (pred[8,256,1]{1,2,0:T(4,128)(4,1)S(1)}, pred[8,256,1]{1,2,0:T(4,128)(4,1)}, u32[]{:S(2)}) copy-start(pred[8,256,1]{1,2,0:T(4,128)(4,1)} %get-tuple-element.225) | copy-start | bytes 6148
  525.0 49.5 %all-to-all-start.4 = ((bf16[8,384,128]{2,0,1:T(8,128)(2,1)}), bf16[8,384,128]{2,0,1:T(8,128)(2,1)}, u32[]{:S(2)}, u32[]{:S(2)}) async-start(bf16[8,384,128]{2,0,1:T(8,128)(2,1)} %copy.166), calls=%async_computation.4 | async-start | bytes 1572864 | tf_op jit(solution)/shard_map/all_to_all | solution.py:101
where the time goes:
time: 594 us; the launch traced here: 590 us
  waiting for transfers between devices  173 us (29%)
  local copies, waits for them, and re-layouts  158 us (27%)
  blocking collectives  103 us (17%)
  starting transfers between devices  79.7 us (13%)
  matrix products  50.3 us (8%)
  other arithmetic  23.6 us (4%)
    gather x5, local copies, waits for them, and re-layouts, pack_rows(): picked = jnp.take_along_axis(head_view, source_row[:, :, None], axis=1)  79.7 us
    all_to_all x1, blocking collectives, body(): lax.all_to_all(packed_query, 'seq', split_axis=1, concat_axis=1, tiled=True)  53.3 us
    all_to_all x1, blocking collectives, body(): lax.all_to_all(packed_key, 'seq', split_axis=1, concat_axis=1, tiled=True)  49.4 us
    gather x4, local copies, waits for them, and re-layouts, unpack_rows(): picked = jnp.take_along_axis(tensor, position[:, :, None], axis=1)  44.6 us
    all_to_all x1, waiting for transfers between devices, body(): lax.all_to_all(results[3], 'seq', split_axis=1, concat_axis=1, tiled=True)  38.1 us
    all_to_all x1, waiting for transfers between devices, body(): lax.all_to_all(results[1], 'seq', split_axis=1, concat_axis=1, tiled=True)  37.9 us
    all_to_all x1, waiting for transfers between devices, body(): lax.all_to_all(packed_value, 'seq', split_axis=1, concat_axis=1, tiled=True)  37.5 us
    all_to_all x1, waiting for transfers between devices, body(): lax.all_to_all(results[2], 'seq', split_axis=1, concat_axis=1, tiled=True)  37 us
  transfers between devices with their start and end apart: 7, of which 6 were waited for; matrix products, arithmetic and copies ran while one was open for 27% of the time, Pallas kernels for 0%

commit v1 on v0

v1 whole, which is shorter than its diff:
```python
import math

import jax
import jax.numpy as jnp
from jax import lax
from jax.experimental import pallas as pl
from jax.experimental.pallas import tpu as pltpu
from jax.sharding import PartitionSpec as P

DEAD_KEY = 256.0
DEAD_TEST = 100.0


def dot_nn(left, right):
    return jnp.dot(left, right, preferred_element_type=jnp.float32)


def dot_nt(left, right):
    return lax.dot_general(left, right, (((1,), (1,)), ((), ())), preferred_element_type=jnp.float32)


def dot_tn(left, right):
    return lax.dot_general(left, right, (((0,), (0,)), ((), ())), preferred_element_type=jnp.float32)


def pack_kernel(routes_ref, q_ref, k_ref, v_ref, g_ref, out_ref, place_ref, scratch, *, owners, slots):
    tokens = routes_ref.shape[2]
    rows = owners * slots
    clusters = routes_ref[0]
    onehot = lax.broadcasted_iota(jnp.int32, (owners, tokens), 0) == clusters
    onehot_low = jnp.where(onehot, 1.0, 0.0).astype(jnp.bfloat16)
    earlier = lax.broadcasted_iota(jnp.int32, (tokens, tokens), 0) < lax.broadcasted_iota(
        jnp.int32, (tokens, tokens), 1
    )
    before = dot_nn(onehot_low, jnp.where(earlier, 1.0, 0.0).astype(jnp.bfloat16))
    ranking = jnp.sum(jnp.where(onehot, before, 0.0), axis=0, keepdims=True)
    place = clusters * slots + ranking.astype(jnp.int32)
    place_ref[0] = place
    select = jnp.where(
        lax.broadcasted_iota(jnp.int32, (rows, tokens), 0) == place, 1.0, 0.0
    ).astype(jnp.bfloat16)
    size = q_ref.shape[1]
    query_key = dot_nn(select, jnp.concatenate([q_ref[...], k_ref[...]], axis=1))
    value_grad = dot_nn(select, jnp.concatenate([v_ref[...], g_ref[...]], axis=1))
    live = dot_nn(select, jnp.ones((tokens, size), jnp.bfloat16))
    scratch[pl.ds(0, rows, stride=4), :] = query_key[:, :size]
    scratch[pl.ds(1, rows, stride=4), :] = query_key[:, size:] + (1.0 - live) * DEAD_KEY
    scratch[pl.ds(2, rows, stride=4), :] = value_grad[:, :size]
    scratch[pl.ds(3, rows, stride=4), :] = value_grad[:, size:]
    out_ref[...] = scratch[...].astype(jnp.bfloat16)


def attention_kernel(in_ref, out_ref, scratch):
    rows = in_ref.shape[0] // 4
    size = in_ref.shape[1]
    scaling = 1.0 / math.sqrt(size)
    scratch[...] = in_ref[...].astype(jnp.float32)
    query, key, value, grad = [
        scratch[pl.ds(i, rows, stride=4), :].astype(jnp.bfloat16) for i in range(4)
    ]
    first_lane = jnp.where(lax.broadcasted_iota(jnp.int32, (8, size), 1) == 0, 1.0, 0.0)
    marks = dot_nt(first_lane.astype(jnp.bfloat16), key)[0:1]
    scores = dot_nt(query, key) * scaling
    masked = jnp.where(marks < DEAD_TEST, scores, -1e30)
    weights = jnp.exp(masked - jnp.max(masked, axis=1, keepdims=True))
    probability = weights * (1.0 / jnp.sum(weights, axis=1, keepdims=True))
    probability_low = probability.astype(jnp.bfloat16)
    output = dot_nn(probability_low, value).astype(jnp.bfloat16)
    grad_probability = dot_nt(grad, value)
    delta = jnp.sum(
        grad.astype(jnp.float32) * output.astype(jnp.float32), axis=1, keepdims=True
    )
    grad_scores = (probability * (grad_probability - delta)).astype(jnp.bfloat16)
    scratch[pl.ds(0, rows, stride=4), :] = output.astype(jnp.float32)
    scratch[pl.ds(1, rows, stride=4), :] = dot_nn(grad_scores, key) * scaling
    scratch[pl.ds(2, rows, stride=4), :] = dot_tn(grad_scores, query) * scaling
    scratch[pl.ds(3, rows, stride=4), :] = dot_tn(probability_low, grad)
    out_ref[...] = scratch[...].astype(jnp.bfloat16)


def unpack_kernel(place_ref, in_ref, o_ref, dq_ref, dk_ref, dv_ref, scratch):
    rows = in_ref.shape[0] // 4
    tokens, size = o_ref.shape
    scratch[...] = in_ref[...].astype(jnp.float32)
    select = jnp.where(
        lax.broadcasted_iota(jnp.int32, (rows, tokens), 0) == place_ref[0], 1.0, 0.0
    ).astype(jnp.bfloat16)
    parts = [scratch[pl.ds(i, rows, stride=4), :].astype(jnp.bfloat16) for i in range(4)]
    first = dot_tn(select, jnp.concatenate(parts[:2], axis=1)).astype(jnp.bfloat16)
    second = dot_tn(select, jnp.concatenate(parts[2:], axis=1)).astype(jnp.bfloat16)
    o_ref[...] = first[:, :size]
    dq_ref[...] = first[:, size:]
    dk_ref[...] = second[:, :size]
    dv_ref[...] = second[:, size:]


def body(queries, key_rows, values, grad_out, routes):
    tokens, features = queries.shape
    heads = routes.shape[0]
    size = features // heads
    owners = lax.axis_size("seq")
    slots = 3 * tokens // (2 * owners)
    rows = owners * slots
    params = pltpu.CompilerParams(
        dimension_semantics=("arbitrary",), vmem_limit_bytes=48 * 1024 * 1024
    )
    head_rows = pl.BlockSpec((tokens, size), lambda h: (0, h))
    head_row = pl.BlockSpec((1, 1, tokens), lambda h: (h, 0, 0))
    packed_block = pl.BlockSpec((4 * rows, size), lambda h: (0, h))
    packed_shape = jax.ShapeDtypeStruct((4 * rows, features), jnp.bfloat16)
    scratch = [pltpu.VMEM((4 * rows, size), jnp.float32)]

    def exchange(packed):
        moved = lax.all_to_all(
            packed.reshape(owners, 4 * slots, features), "seq", split_axis=0, concat_axis=0, tiled=True
        )
        return moved.reshape(4 * rows, features)

    packed, place = pl.pallas_call(
        lambda *refs: pack_kernel(*refs, owners=owners, slots=slots),
        grid=(heads,),
        in_specs=[head_row, head_rows, head_rows, head_rows, head_rows],
        out_specs=[packed_block, head_row],
        out_shape=[packed_shape, jax.ShapeDtypeStruct((heads, 1, tokens), jnp.int32)],
        scratch_shapes=scratch,
        compiler_params=params,
        name="pack_rows",
    )(routes.reshape(heads, 1, tokens), queries, key_rows, values, grad_out)
    results = pl.pallas_call(
        attention_kernel,
        grid=(heads,),
        in_specs=[packed_block],
        out_specs=packed_block,
        out_shape=packed_shape,
        scratch_shapes=scratch,
        compiler_params=params,
        name="cluster_attention",
    )(exchange(packed))
    return tuple(
        pl.pallas_call(
            unpack_kernel,
            grid=(heads,),
            in_specs=[head_row, packed_block],
            out_specs=[head_rows] * 4,
            out_shape=[jax.ShapeDtypeStruct((tokens, features), jnp.bfloat16)] * 4,
            scratch_shapes=scratch,
            compiler_params=params,
            name="unpack_rows",
        )(place, exchange(results))
    )


def solution(mesh):
    in_specs = (
        P("seq", "head"),
        P("seq", "head"),
        P("seq", "head"),
        P("seq", "head"),
        P("head", "seq", None),
    )
    out_specs = (P("seq", "head"), P("seq", "head"), P("seq", "head"), P("seq", "head"))
    return jax.shard_map(body, mesh=mesh, in_specs=in_specs, out_specs=out_specs, check_vma=False)
```

time: 594 us -> 341 us (0.57)
  blocking collectives: 103 us -> 310 us
  waiting for transfers between devices: 173 us -> 0 us
  local copies, waits for them, and re-layouts: 158 us -> 4.85 us
  starting transfers between devices: 79.7 us -> 0 us
  matrix products: 50.3 us -> 0 us
  other arithmetic: 23.6 us -> 0 us
  Pallas kernels: 0 us -> 21.9 us
    all_to_all x2, blocking collectives: 103 us -> 310 us  [exchange(): lax.all_to_all(packed.reshape(owners, 4 * slots, features), 'seq', split_...]
    all_to_all x7 -> x0, waiting for transfers between devices: 173 us -> none  [the longest x1 38.1 us: body(): lax.all_to_all(results[3], 'seq', split_axis=1, concat_axis=1, tiled=True)]
    gather x9 -> x0, local copies, waits for them, and re-layouts: 124 us -> none  [the longest x5 79.7 us: pack_rows(): picked = jnp.take_along_axis(head_view, source_row[:, :, None], axis=1)]
    all_to_all x7 -> x0, starting transfers between devices: 79.7 us -> none  [the longest x1 19.2 us: body(): lax.all_to_all(counts, 'seq', split_axis=1, concat_axis=1, tiled=True)]
    dot_general x49 -> x0, matrix products: 50.3 us -> none  [the longest x8 14.2 us: backward_head(): jnp.dot(grad_scores, key_block, preferred_element_type=jnp.float32)]
    pallas_call x0 -> x3, Pallas kernels: none -> 21.9 us  [the longest x1 10.9 us: body(): pl.pallas_call(attention_kernel, grid=(heads,), in_specs=[packed_block],...]
    select_n x2 -> x0, other arithmetic: 11 us -> none  [the longest x1 11 us: pack_rows(): return jnp.where(filled[:, :, None], picked, jnp.zeros_like(picked))]
    dynamic_slice x24 -> x0, local copies, waits for them, and re-layouts: 10.9 us -> none  [the longest x16 10.7 us: cluster_work(): lax.map(backward_head, (query_rows, key_part, value_rows, grad_rows, prob...]
  transfers between devices with their start and end apart: 7 -> 0, of which waited for: 6 -> 0; matrix products, arithmetic and copies ran while one was open for 27% -> 0% of each run, Pallas kernels for 0% -> 0%
where the time goes in v1:
time: 341 us; the launch traced here: 337 us
  blocking collectives  310 us (91%)
  Pallas kernels  21.9 us (6%)
  local copies, waits for them, and re-layouts  4.85 us (1%)
    all_to_all x2, blocking collectives, exchange(): lax.all_to_all(packed.reshape(owners, 4 * slots, features), 'seq', split_...  310 us
    pallas_call x1, Pallas kernels, body(): pl.pallas_call(attention_kernel, grid=(heads,), in_specs=[packed_block],...  10.9 us

profile of v1, /device:TPU:1, one launch (start us, length us, event | category | flops | bytes accessed | tf_op | source)
XLA Modules:
  0.0 337.2 jit_solution(10308103542915369225)
XLA Ops:
  0.6 0.0 copy-start
  0.6 1.0 copy-done
  1.7 0.0 copy-start.1
  1.7 1.0 copy-done.1
  2.7 0.0 copy-start.2
  2.7 1.0 copy-done.2
  3.8 0.0 copy-start.3
  3.8 1.0 copy-done.3
  4.8 0.0 copy-start.4
  4.8 0.7 copy-done.4
  5.5 5.8 %pack_rows.1 = (bf16[1536,1024]{1,0:T(8,128)(2,1)S(1)}, s32[8,1,256]{2,1,0:T(1,128)S(1)}) custom-call(s32[8,1,256]{2,1,0:T(1,128)S(1)} %bitcast.8, bf16[256,1024]{1,0:T(8,128)(2,1)S(1)} %copy-done, bf16[256,1024]{1,0:T(8,128)(2,1)S(1)} %copy-done.1, bf16[256,1024]{1,0:T(8,128)(2,1)S(1)} %copy-done.2, bf16[256,1024]{1,0:T(8,128)(2,1)S(1)} %copy-done.3), custom_call_target="tpu_custom_call" | custom-call | tf_op jit(solution)/shard_map/pack_rows/pallas_call | solution.py:119
  11.3 159.2 %all_to_all.10 = bf16[64,24,1024]{2,1,0:T(8,128)(2,1)} all-to-all(bf16[64,24,1024]{2,1,0:T(8,128)(2,1)S(1)} %bitcast.7), channel_id=1, replica_groups=mesh['seq'=64,'head'=8] {'seq'}, dimensions={0} | all-to-all | bytes 6291456 | tf_op jit(solution)/shard_map/all_to_all | solution.py:114
  170.5 10.9 %cluster_attention.1 = bf16[1536,1024]{1,0:T(8,128)(2,1)S(1)} custom-call(bf16[1536,1024]{1,0:T(8,128)(2,1)} %bitcast.9), custom_call_target="tpu_custom_call" | custom-call | tf_op jit(solution)/shard_map/cluster_attention/pallas_call | solution.py:129
  181.5 150.6 %all_to_all.11 = bf16[64,24,1024]{2,1,0:T(8,128)(2,1)S(1)} all-to-all(bf16[64,24,1024]{2,1,0:T(8,128)(2,1)S(1)} %bitcast.6), channel_id=1, replica_groups=mesh['seq'=64,'head'=8] {'seq'}, dimensions={0} | all-to-all | bytes 6291456 | tf_op jit(solution)/shard_map/all_to_all | solution.py:114
  332.0 5.2 %unpack_rows.1 = (bf16[256,1024]{1,0:T(8,128)(2,1)}, bf16[256,1024]{1,0:T(8,128)(2,1)}, bf16[256,1024]{1,0:T(8,128)(2,1)}, bf16[256,1024]{1,0:T(8,128)(2,1)}) custom-call(s32[8,1,256]{2,1,0:T(1,128)S(1)} %get-tuple-element.6.place_ref, bf16[1536,1024]{1,0:T(8,128)(2,1)S(1)} %bitcast.5), custom_call_target="tpu_custom_call" | custom-call | tf_op jit(solution)/shard_map/unpack_rows/pallas_call | solution.py:140
Async XLA Ops:
  0.6 1.0 copy-start
  1.7 1.0 copy-start.1
  2.7 1.0 copy-start.2
  3.8 1.0 copy-start.3
  4.8 0.7 copy-start.4

commit v2 on v1

v2 whole, which is shorter than its diff:
```python
import math

import jax
import jax.numpy as jnp
from jax import lax
from jax.experimental import pallas as pl
from jax.experimental.pallas import tpu as pltpu
from jax.sharding import PartitionSpec as P

DEAD_KEY = 256.0
DEAD_TEST = 100.0
PACK_HEADS = 4
ATTEND_HEADS = 2
UNPACK_HEADS = 4


def dot_nn(left, right):
    return jnp.dot(left, right, preferred_element_type=jnp.float32)


def dot_nt(left, right):
    return lax.dot_general(left, right, (((1,), (1,)), ((), ())), preferred_element_type=jnp.float32)


def dot_tn(left, right):
    return lax.dot_general(left, right, (((0,), (0,)), ((), ())), preferred_element_type=jnp.float32)


def pack_kernel(routes_ref, q_ref, k_ref, v_ref, g_ref, out_ref, place_ref, scratch, *, owners, slots):
    group, _, tokens = routes_ref.shape
    rows = owners * slots
    size = q_ref.shape[1] // group
    earlier = lax.broadcasted_iota(jnp.int32, (tokens, tokens), 0) < lax.broadcasted_iota(
        jnp.int32, (tokens, tokens), 1
    )
    earlier_low = jnp.where(earlier, 1.0, 0.0).astype(jnp.bfloat16)
    owner_ids = lax.broadcasted_iota(jnp.int32, (owners, tokens), 0)
    row_ids = lax.broadcasted_iota(jnp.int32, (rows, tokens), 0)
    for j in range(group):
        lanes = slice(j * size, (j + 1) * size)
        clusters = routes_ref[j]
        onehot = owner_ids == clusters
        before = dot_nn(jnp.where(onehot, 1.0, 0.0).astype(jnp.bfloat16), earlier_low)
        ranking = jnp.sum(jnp.where(onehot, before, 0.0), axis=0, keepdims=True)
        place = clusters * slots + ranking.astype(jnp.int32)
        place_ref[j] = place
        select = jnp.where(row_ids == place, 1.0, 0.0).astype(jnp.bfloat16)
        query_key = dot_nn(select, jnp.concatenate([q_ref[:, lanes], k_ref[:, lanes]], axis=1))
        value_grad = dot_nn(select, jnp.concatenate([v_ref[:, lanes], g_ref[:, lanes]], axis=1))
        live = dot_nn(select, jnp.ones((tokens, size), jnp.bfloat16))
        scratch[j, pl.ds(0, rows, stride=4), :] = query_key[:, :size]
        scratch[j, pl.ds(1, rows, stride=4), :] = query_key[:, size:] + (1.0 - live) * DEAD_KEY
        scratch[j, pl.ds(2, rows, stride=4), :] = value_grad[:, :size]
        scratch[j, pl.ds(3, rows, stride=4), :] = value_grad[:, size:]
        out_ref[:, lanes] = scratch[j].astype(jnp.bfloat16)


def attention_kernel(in_ref, out_ref, scratch, scratch_out):
    rows = in_ref.shape[0] // 4
    group = scratch.shape[0]
    size = in_ref.shape[1] // group
    scaling = 1.0 / math.sqrt(size)
    first_lane = jnp.where(lax.broadcasted_iota(jnp.int32, (8, size), 1) == 0, 1.0, 0.0)
    first_lane = first_lane.astype(jnp.bfloat16)
    for j in range(group):
        lanes = slice(j * size, (j + 1) * size)
        scratch[j] = in_ref[:, lanes].astype(jnp.float32)
        query, key, value, grad = [
            scratch[j, pl.ds(i, rows, stride=4), :].astype(jnp.bfloat16) for i in range(4)
        ]
        marks = dot_nt(first_lane, key)[0:1]
        scores = dot_nt(query, key) * scaling
        masked = jnp.where(marks < DEAD_TEST, scores, -1e30)
        weights = jnp.exp(masked - jnp.max(masked, axis=1, keepdims=True))
        probability = weights * (1.0 / jnp.sum(weights, axis=1, keepdims=True))
        probability_low = probability.astype(jnp.bfloat16)
        output = dot_nn(probability_low, value).astype(jnp.bfloat16)
        grad_probability = dot_nt(grad, value)
        delta = jnp.sum(
            grad.astype(jnp.float32) * output.astype(jnp.float32), axis=1, keepdims=True
        )
        grad_scores = (probability * (grad_probability - delta)).astype(jnp.bfloat16)
        scratch_out[j, pl.ds(0, rows, stride=4), :] = output.astype(jnp.float32)
        scratch_out[j, pl.ds(1, rows, stride=4), :] = dot_nn(grad_scores, key) * scaling
        scratch_out[j, pl.ds(2, rows, stride=4), :] = dot_tn(grad_scores, query) * scaling
        scratch_out[j, pl.ds(3, rows, stride=4), :] = dot_tn(probability_low, grad)
        out_ref[:, lanes] = scratch_out[j].astype(jnp.bfloat16)


def unpack_kernel(place_ref, in_ref, o_ref, dq_ref, dk_ref, dv_ref, scratch):
    rows = in_ref.shape[0] // 4
    group, _, tokens = place_ref.shape
    size = o_ref.shape[1] // group
    row_ids = lax.broadcasted_iota(jnp.int32, (rows, tokens), 0)
    for j in range(group):
        lanes = slice(j * size, (j + 1) * size)
        scratch[j] = in_ref[:, lanes].astype(jnp.float32)
        select = jnp.where(row_ids == place_ref[j], 1.0, 0.0).astype(jnp.bfloat16)
        parts = [scratch[j, pl.ds(i, rows, stride=4), :].astype(jnp.bfloat16) for i in range(4)]
        first = dot_tn(select, jnp.concatenate(parts[:2], axis=1)).astype(jnp.bfloat16)
        second = dot_tn(select, jnp.concatenate(parts[2:], axis=1)).astype(jnp.bfloat16)
        o_ref[:, lanes] = first[:, :size]
        dq_ref[:, lanes] = first[:, size:]
        dk_ref[:, lanes] = second[:, :size]
        dv_ref[:, lanes] = second[:, size:]


def build(tokens, features, heads, owners):
    size = features // heads
    slots = 3 * tokens // (2 * owners)
    rows = owners * slots
    params = pltpu.CompilerParams(
        dimension_semantics=("arbitrary",), vmem_limit_bytes=56 * 1024 * 1024
    )
    packed_shape = jax.ShapeDtypeStruct((4 * rows, features), jnp.bfloat16)

    def head_rows(group):
        return pl.BlockSpec((tokens, group * size), lambda h: (0, h))

    def head_row(group):
        return pl.BlockSpec((group, 1, tokens), lambda h: (h, 0, 0))

    def packed_block(group):
        return pl.BlockSpec((4 * rows, group * size), lambda h: (0, h))

    def scratch(group):
        return pltpu.VMEM((group, 4 * rows, size), jnp.float32)

    pack = pl.pallas_call(
        lambda *refs: pack_kernel(*refs, owners=owners, slots=slots),
        grid=(heads // PACK_HEADS,),
        in_specs=[head_row(PACK_HEADS)] + [head_rows(PACK_HEADS)] * 4,
        out_specs=[packed_block(PACK_HEADS), head_row(PACK_HEADS)],
        out_shape=[packed_shape, jax.ShapeDtypeStruct((heads, 1, tokens), jnp.int32)],
        scratch_shapes=[scratch(PACK_HEADS)],
        compiler_params=params,
        name="pack_rows",
    )
    attend = pl.pallas_call(
        attention_kernel,
        grid=(heads // ATTEND_HEADS,),
        in_specs=[packed_block(ATTEND_HEADS)],
        out_specs=packed_block(ATTEND_HEADS),
        out_shape=packed_shape,
        scratch_shapes=[scratch(ATTEND_HEADS)] * 2,
        compiler_params=params,
        name="cluster_attention",
    )
    unpack = pl.pallas_call(
        unpack_kernel,
        grid=(heads // UNPACK_HEADS,),
        in_specs=[head_row(UNPACK_HEADS), packed_block(UNPACK_HEADS)],
        out_specs=[head_rows(UNPACK_HEADS)] * 4,
        out_shape=[jax.ShapeDtypeStruct((tokens, features), jnp.bfloat16)] * 4,
        scratch_shapes=[scratch(UNPACK_HEADS)],
        compiler_params=params,
        name="unpack_rows",
    )
    return pack, attend, unpack


def body(queries, key_rows, values, grad_out, routes):
    tokens, features = queries.shape
    heads = routes.shape[0]
    owners = lax.axis_size("seq")
    pack, attend, unpack = build(tokens, features, heads, owners)

    def exchange(packed):
        moved = lax.all_to_all(
            packed.reshape(owners, -1, features), "seq", split_axis=0, concat_axis=0, tiled=True
        )
        return moved.reshape(packed.shape)

    def in_hbm(array):
        return pltpu.with_memory_space_constraint(array, pltpu.HBM)

    packed, place = pack(
        routes.reshape(heads, 1, tokens),
        in_hbm(queries),
        in_hbm(key_rows),
        in_hbm(values),
        in_hbm(grad_out),
    )
    results = attend(exchange(packed))
    return tuple(unpack(place, exchange(results)))


def solution(mesh):
    in_specs = (
        P("seq", "head"),
        P("seq", "head"),
        P("seq", "head"),
        P("seq", "head"),
        P("head", "seq", None),
    )
    out_specs = (P("seq", "head"), P("seq", "head"), P("seq", "head"), P("seq", "head"))
    return jax.shard_map(body, mesh=mesh, in_specs=in_specs, out_specs=out_specs, check_vma=False)
```

time: 341 us -> 334 us (0.979)
  local copies, waits for them, and re-layouts: 4.85 us -> 0 us
    unnamed x10 -> x0, local copies, waits for them, and re-layouts: 4.85 us -> none
where the time goes in v2:
time: 334 us; the launch traced here: 331 us
  blocking collectives  310 us (93%)
  Pallas kernels  19.6 us (6%)
    all_to_all x2, blocking collectives, exchange(): lax.all_to_all(packed.reshape(owners, -1, features), 'seq', split_axis=0,...  310 us
    pallas_call x1, Pallas kernels, body(): results = attend(exchange(packed))  10.2 us

profile of v2, /device:TPU:1, one launch (start us, length us, event | category | flops | bytes accessed | tf_op | source)
XLA Modules:
  0.0 330.6 jit_solution(8621086866392652769)
XLA Ops:
  0.6 5.5 %pack_rows.1 = (bf16[1536,1024]{1,0:T(8,128)(2,1)}, s32[8,1,256]{2,1,0:T(1,128)}) custom-call(s32[8,1,256]{2,1,0:T(1,128)} %bitcast.9, bf16[256,1024]{1,0:T(8,128)(2,1)} %refs_1_.1, bf16[256,1024]{1,0:T(8,128)(2,1)} %refs_2_.1, bf16[256,1024]{1,0:T(8,128)(2,1)} %refs_3_.1, bf16[256,1024]{1,0:T(8,128)(2,1)} %refs_4_.1), custom_call_target="tpu_custom_call" | custom-call | tf_op jit(solution)/shard_map/pack_rows/pallas_call | solution.py:177
  6.1 159.4 %all_to_all.10 = bf16[64,24,1024]{2,1,0:T(8,128)(2,1)} all-to-all(bf16[64,24,1024]{2,1,0:T(8,128)(2,1)} %bitcast.8), channel_id=1, replica_groups=mesh['seq'=64,'head'=8] {'seq'}, dimensions={0} | all-to-all | bytes 6291456 | tf_op jit(solution)/shard_map/all_to_all | solution.py:169
  165.5 10.2 %cluster_attention.1 = bf16[1536,1024]{1,0:T(8,128)(2,1)} custom-call(bf16[1536,1024]{1,0:T(8,128)(2,1)} %bitcast.6), custom_call_target="tpu_custom_call" | custom-call | tf_op jit(solution)/shard_map/cluster_attention/pallas_call | solution.py:184
  175.7 150.9 %all_to_all.11 = bf16[64,24,1024]{2,1,0:T(8,128)(2,1)} all-to-all(bf16[64,24,1024]{2,1,0:T(8,128)(2,1)} %bitcast.7), channel_id=1, replica_groups=mesh['seq'=64,'head'=8] {'seq'}, dimensions={0} | all-to-all | bytes 6291456 | tf_op jit(solution)/shard_map/all_to_all | solution.py:169
  326.6 4.0 %unpack_rows.1 = (bf16[256,1024]{1,0:T(8,128)(2,1)}, bf16[256,1024]{1,0:T(8,128)(2,1)}, bf16[256,1024]{1,0:T(8,128)(2,1)}, bf16[256,1024]{1,0:T(8,128)(2,1)}) custom-call(s32[8,1,256]{2,1,0:T(1,128)} %get-tuple-element.6.place_ref, bf16[1536,1024]{1,0:T(8,128)(2,1)} %bitcast.5), custom_call_target="tpu_custom_call" | custom-call | tf_op jit(solution)/shard_map/unpack_rows/pallas_call | solution.py:185

commit v3 on v2

--- a/solution.py
+++ b/solution.py
@@ -9,6 +9,10 @@
 
 DEAD_KEY = 256.0
 DEAD_TEST = 100.0
+MESSAGE_ROWS = 44
+OWNED = 8
+WIDE = 8
+SOURCES = 4
 PACK_HEADS = 4
 ATTEND_HEADS = 2
 UNPACK_HEADS = 4
@@ -55,35 +59,38 @@
         out_ref[:, lanes] = scratch[j].astype(jnp.bfloat16)
 
 
+def attend_cluster(query, key, value, grad):
+    size = query.shape[1]
+    scaling = 1.0 / math.sqrt(size)
+    first_lane = jnp.where(lax.broadcasted_iota(jnp.int32, (8, size), 1) == 0, 1.0, 0.0)
+    marks = dot_nt(first_lane.astype(jnp.bfloat16), key)[0:1]
+    scores = dot_nt(query, key) * scaling
+    masked = jnp.where(marks < DEAD_TEST, scores, -1e30)
+    weights = jnp.exp(masked - jnp.max(masked, axis=1, keepdims=True))
+    probability = weights * (1.0 / jnp.sum(weights, axis=1, keepdims=True))
+    probability_low = probability.astype(jnp.bfloat16)
+    output = dot_nn(probability_low, value).astype(jnp.bfloat16).astype(jnp.float32)
+    grad_probability = dot_nt(grad, value)
+    delta = jnp.sum(grad.astype(jnp.float32) * output, axis=1, keepdims=True)
+    grad_scores = (probability * (grad_probability - delta)).astype(jnp.bfloat16)
+    return (
+        output,
+        dot_nn(grad_scores, key) * scaling,
+        dot_tn(grad_scores, query) * scaling,
+        dot_tn(probability_low, grad),
+    )
+
+
 def attention_kernel(in_ref, out_ref, scratch, scratch_out):
     rows = in_ref.shape[0] // 4
     group = scratch.shape[0]
     size = in_ref.shape[1] // group
-    scaling = 1.0 / math.sqrt(size)
-    first_lane = jnp.where(lax.broadcasted_iota(jnp.int32, (8, size), 1) == 0, 1.0, 0.0)
-    first_lane = first_lane.astype(jnp.bfloat16)
     for j in range(group):
         lanes = slice(j * size, (j + 1) * size)
         scratch[j] = in_ref[:, lanes].astype(jnp.float32)
-        query, key, value, grad = [
-            scratch[j, pl.ds(i, rows, stride=4), :].astype(jnp.bfloat16) for i in range(4)
-        ]
-        marks = dot_nt(first_lane, key)[0:1]
-        scores = dot_nt(query, key) * scaling
-        masked = jnp.where(marks < DEAD_TEST, scores, -1e30)
-        weights = jnp.exp(masked - jnp.max(masked, axis=1, keepdims=True))
-        probability = weights * (1.0 / jnp.sum(weights, axis=1, keepdims=True))
-        probability_low = probability.astype(jnp.bfloat16)
-        output = dot_nn(probability_low, value).astype(jnp.bfloat16)
-        grad_probability = dot_nt(grad, value)
-        delta = jnp.sum(
-            grad.astype(jnp.float32) * output.astype(jnp.float32), axis=1, keepdims=True
-        )
-        grad_scores = (probability * (grad_probability - delta)).astype(jnp.bfloat16)
-        scratch_out[j, pl.ds(0, rows, stride=4), :] = output.astype(jnp.float32)
-        scratch_out[j, pl.ds(1, rows, stride=4), :] = dot_nn(grad_scores, key) * scaling
-        scratch_out[j, pl.ds(2, rows, stride=4), :] = dot_tn(grad_scores, query) * scaling
-        scratch_out[j, pl.ds(3, rows, stride=4), :] = dot_tn(probability_low, grad)
+        tensors = [scratch[j, pl.ds(i, rows, stride=4), :].astype(jnp.bfloat16) for i in range(4)]
+        for i, result in enumerate(attend_cluster(*tensors)):
+            scratch_out[j, pl.ds(i, rows, stride=4), :] = result
         out_ref[:, lanes] = scratch_out[j].astype(jnp.bfloat16)
 
 
@@ -105,12 +112,137 @@
         dv_ref[:, lanes] = second[:, size:]
 
 
+def dense_pack_kernel(
+    routes_ref, q_ref, k_ref, v_ref, g_ref, out_ref, place_ref, counts_ref, scratch, *, clusters
+):
+    group, _, tokens = routes_ref.shape
+    rows = scratch.shape[1] // 4
+    size = q_ref.shape[1] // group
+    earlier = lax.broadcasted_iota(jnp.int32, (tokens, tokens), 0) < lax.broadcasted_iota(
+        jnp.int32, (tokens, tokens), 1
+    )
+    earlier_low = jnp.where(earlier, 1.0, 0.0).astype(jnp.bfloat16)
+    this = lax.broadcasted_iota(jnp.int32, (clusters, clusters), 0)
+    other = lax.broadcasted_iota(jnp.int32, (clusters, clusters), 1)
+    lower = jnp.logical_and(other < this, other // OWNED == this // OWNED)
+    lower_low = jnp.where(lower, 1.0, 0.0).astype(jnp.bfloat16)
+    all_tokens = jnp.ones((tokens, tokens), jnp.bfloat16)
+    cluster_ids = lax.broadcasted_iota(jnp.int32, (clusters, tokens), 0)
+    row_ids = lax.broadcasted_iota(jnp.int32, (rows, tokens), 0)
+    for j in range(group):
+        lanes = slice(j * size, (j + 1) * size)
+        route = routes_ref[j]
+        onehot = cluster_ids == route
+        onehot_low = jnp.where(onehot, 1.0, 0.0).astype(jnp.bfloat16)
+        counts_ref[j] = dot_nt(all_tokens[:8], onehot_low)[0:1].astype(jnp.int32)
+        in_lower = dot_nn(lower_low, onehot_low).astype(jnp.bfloat16)
+        before = dot_nn(onehot_low, earlier_low) + dot_nn(in_lower, all_tokens)
+        ranking = jnp.sum(jnp.where(onehot, before, 0.0), axis=0, keepdims=True)
+        place = route // OWNED * MESSAGE_ROWS + ranking.astype(jnp.int32)
+        place_ref[j] = place
+        select = jnp.where(row_ids == place, 1.0, 0.0).astype(jnp.bfloat16)
+        query_key = dot_nn(select, jnp.concatenate([q_ref[:, lanes], k_ref[:, lanes]], axis=1))
+        value_grad = dot_nn(select, jnp.concatenate([v_ref[:, lanes], g_ref[:, lanes]], axis=1))
+        scratch[j, pl.ds(0, rows, stride=4), :] = query_key[:, :size]
+        scratch[j, pl.ds(1, rows, stride=4), :] = query_key[:, size:]
+        scratch[j, pl.ds(2, rows, stride=4), :] = value_grad[:, :size]
+        scratch[j, pl.ds(3, rows, stride=4), :] = value_grad[:, size:]
+        out_ref[j * 4 * rows : (j + 1) * 4 * rows, :] = scratch[j].astype(jnp.bfloat16)
+
+
+def dense_attention_kernel(counts_ref, in_ref, out_ref, target_ref, stage, wide_ref):
+    size = in_ref.shape[1]
+    steps, pairs = counts_ref.shape
+    count = SOURCES * MESSAGE_ROWS
+    wide = pairs * WIDE
+    sources = steps * SOURCES
+    slots = wide_ref.shape[1] // (sources * OWNED) - 2
+    lanes = lax.broadcasted_iota(jnp.int32, (pairs, wide), 1) // WIDE
+    pair = lax.broadcasted_iota(jnp.int32, (pairs, wide), 0)
+    counts_low = counts_ref[...].astype(jnp.bfloat16)
+    same = jnp.where(lanes == pair, 1.0, 0.0).astype(jnp.bfloat16)
+    ahead = jnp.logical_and(pair < lanes, pair // OWNED == lanes // OWNED)
+    ahead = jnp.where(ahead, 1.0, 0.0).astype(jnp.bfloat16)
+    lane = lax.broadcasted_iota(jnp.int32, (steps, wide), 1)
+    slot = lane % WIDE
+    target = dot_nn(counts_low, ahead).astype(jnp.int32) + slot
+    target = target + lane // (OWNED * WIDE) * MESSAGE_ROWS
+    target_ref[...] = jnp.where(slot < dot_nn(counts_low, same).astype(jnp.int32), target, -1)
+    row_ids = lax.broadcasted_iota(jnp.int32, (count, wide), 0)
+    ones = jnp.ones((count, size), jnp.bfloat16)
+
+    def selection(step):
+        return jnp.where(row_ids == target_ref[pl.ds(step, 1), :], 1.0, 0.0).astype(jnp.bfloat16)
+
+    def expand(pass_id, carry):
+        for u in range(stage.shape[0]):
+            step = pass_id * stage.shape[0] + u
+            stage[u] = in_ref[pl.ds(step * 4 * count, 4 * count), :].astype(jnp.float32)
+            parts = [stage[u, pl.ds(i, count, stride=4), :].astype(jnp.bfloat16) for i in range(4)]
+            select = selection(step)
+            into = pl.ds(step * wide, wide)
+            query_key = dot_tn(select, jnp.concatenate(parts[:2], axis=1))
+            value_grad = dot_tn(select, jnp.concatenate(parts[2:], axis=1))
+            live = dot_tn(select, ones)
+            wide_ref[0, into, :] = query_key[:, :size]
+            wide_ref[1, into, :] = query_key[:, size:] + (1.0 - live) * DEAD_KEY
+            wide_ref[2, into, :] = value_grad[:, :size]
+            wide_ref[3, into, :] = value_grad[:, size:]
+        return carry
+
+    def compact(pass_id, carry):
+        for u in range(stage.shape[0]):
+            step = pass_id * stage.shape[0] + u
+            select = selection(step)
+            parts = [
+                wide_ref[i, pl.ds(step * wide, wide), :].astype(jnp.bfloat16) for i in range(4)
+            ]
+            first = dot_nn(select, jnp.concatenate(parts[:2], axis=1))
+            second = dot_nn(select, jnp.concatenate(parts[2:], axis=1))
+            stage[u, pl.ds(0, count, stride=4), :] = first[:, :size]
+            stage[u, pl.ds(1, count, stride=4), :] = first[:, size:]
+            stage[u, pl.ds(2, count, stride=4), :] = second[:, :size]
+            stage[u, pl.ds(3, count, stride=4), :] = second[:, size:]
+            out_ref[pl.ds(step * 4 * count, 4 * count), :] = stage[u].astype(jnp.bfloat16)
+        return carry
+
+    lax.fori_loop(0, steps // stage.shape[0], expand, 0)
+    for c in range(OWNED):
+        spots = [pl.ds(c * WIDE + s, sources, stride=OWNED * WIDE) for s in range(slots)]
+        tensors = [
+            jnp.concatenate([wide_ref[i, spot, :] for spot in spots], axis=0).astype(jnp.bfloat16)
+            for i in range(4)
+        ]
+        for i, result in enumerate(attend_cluster(*tensors)):
+            for s, spot in enumerate(spots):
+                wide_ref[i, spot, :] = result[s * sources : (s + 1) * sources]
+    lax.fori_loop(0, steps // stage.shape[0], compact, 0)
+
+
+def dense_unpack_kernel(place_ref, in_ref, o_ref, dq_ref, dk_ref, dv_ref, scratch):
+    rows = scratch.shape[1] // 4
+    group, _, tokens = place_ref.shape
+    size = o_ref.shape[1] // group
+    row_ids = lax.broadcasted_iota(jnp.int32, (rows, tokens), 0)
+    for j in range(group):
+        lanes = slice(j * size, (j + 1) * size)
+        scratch[j] = in_ref[j * 4 * rows : (j + 1) * 4 * rows, :].astype(jnp.float32)
+        select = jnp.where(row_ids == place_ref[j], 1.0, 0.0).astype(jnp.bfloat16)
+        parts = [scratch[j, pl.ds(i, rows, stride=4), :].astype(jnp.bfloat16) for i in range(4)]
+        first = dot_tn(select, jnp.concatenate(parts[:2], axis=1)).astype(jnp.bfloat16)
+        second = dot_tn(select, jnp.concatenate(parts[2:], axis=1)).astype(jnp.bfloat16)
+        o_ref[:, lanes] = first[:, :size]
+        dq_ref[:, lanes] = first[:, size:]
+        dk_ref[:, lanes] = second[:, :size]
+        dv_ref[:, lanes] = second[:, size:]
+
+
 def build(tokens, features, heads, owners):
     size = features // heads
     slots = 3 * tokens // (2 * owners)
     rows = owners * slots
     params = pltpu.CompilerParams(
-        dimension_semantics=("arbitrary",), vmem_limit_bytes=56 * 1024 * 1024
+        dimension_semantics=("arbitrary",), vmem_limit_bytes=40 * 1024 * 1024
     )
     packed_shape = jax.ShapeDtypeStruct((4 * rows, features), jnp.bfloat16)
 
@@ -159,30 +291,108 @@
     return pack, attend, unpack
 
 
+def build_dense(tokens, features, heads, owners):
+    size = features // heads
+    clusters = heads * OWNED
+    rows = OWNED * MESSAGE_ROWS
+    slots = 3 * tokens // (2 * owners)
+    steps = owners // SOURCES
+    params = pltpu.CompilerParams(
+        dimension_semantics=("arbitrary",), vmem_limit_bytes=40 * 1024 * 1024
+    )
+    packed_shape = jax.ShapeDtypeStruct((heads * 4 * rows, size), jnp.bfloat16)
+
+    def head_rows(group):
+        return pl.BlockSpec((tokens, group * size), lambda h: (0, h))
+
+    def head_row(group, length):
+        return pl.BlockSpec((group, 1, length), lambda h: (h, 0, 0))
+
+    def packed_block(group):
+        return pl.BlockSpec((group * 4 * rows, size), lambda h: (h, 0))
+
+    def scratch(group):
+        return pltpu.VMEM((group, 4 * rows, size), jnp.float32)
+
+    pack = pl.pallas_call(
+        lambda *refs: dense_pack_kernel(*refs, clusters=clusters),
+        grid=(heads // PACK_HEADS,),
+        in_specs=[head_row(PACK_HEADS, tokens)] + [head_rows(PACK_HEADS)] * 4,
+        out_specs=[
+            packed_block(PACK_HEADS),
+            head_row(PACK_HEADS, tokens),
+            head_row(PACK_HEADS, clusters),
+        ],
+        out_shape=[
+            packed_shape,
+            jax.ShapeDtypeStruct((heads, 1, tokens), jnp.int32),
+            jax.ShapeDtypeStruct((heads, 1, clusters), jnp.int32),
+        ],
+        scratch_shapes=[scratch(PACK_HEADS)],
+        compiler_params=params,
+        name="dense_pack_rows",
+    )
+    attend = pl.pallas_call(
+        dense_attention_kernel,
+        out_shape=packed_shape,
+        scratch_shapes=[
+            pltpu.VMEM((steps, SOURCES * OWNED * WIDE), jnp.int32),
+            pltpu.VMEM((2, 4 * SOURCES * MESSAGE_ROWS, size), jnp.float32),
+            pltpu.VMEM((4, owners * OWNED * WIDE, size), jnp.float32),
+        ],
+        compiler_params=pltpu.CompilerParams(vmem_limit_bytes=40 * 1024 * 1024),
+        name="dense_cluster_attention",
+    )
+    unpack = pl.pallas_call(
+        dense_unpack_kernel,
+        grid=(heads // UNPACK_HEADS,),
+        in_specs=[head_row(UNPACK_HEADS, tokens), packed_block(UNPACK_HEADS)],
+        out_specs=[head_rows(UNPACK_HEADS)] * 4,
+        out_shape=[jax.ShapeDtypeStruct((tokens, features), jnp.bfloat16)] * 4,
+        scratch_shapes=[scratch(UNPACK_HEADS)],
+        compiler_params=params,
+        name="dense_unpack_rows",
+    )
+    return pack, attend, unpack
+
+
+def exchange(packed, owners):
+    moved = lax.all_to_all(
+        packed.reshape(owners, -1, packed.shape[1]), "seq", split_axis=0, concat_axis=0, tiled=True
+    )
+    return moved.reshape(packed.shape)
+
+
 def body(queries, key_rows, values, grad_out, routes):
     tokens, features = queries.shape
     heads = routes.shape[0]
     owners = lax.axis_size("seq")
-    pack, attend, unpack = build(tokens, features, heads, owners)
-
-    def exchange(packed):
-        moved = lax.all_to_all(
-            packed.reshape(owners, -1, features), "seq", split_axis=0, concat_axis=0, tiled=True
-        )
-        return moved.reshape(packed.shape)
-
-    def in_hbm(array):
-        return pltpu.with_memory_space_constraint(array, pltpu.HBM)
-
-    packed, place = pack(
-        routes.reshape(heads, 1, tokens),
-        in_hbm(queries),
-        in_hbm(key_rows),
-        in_hbm(values),
-        in_hbm(grad_out),
-    )
-    results = attend(exchange(packed))
-    return tuple(unpack(place, exchange(results)))
+    tensors = [
+        pltpu.with_memory_space_constraint(array, pltpu.HBM)
+        for array in (queries, key_rows, values, grad_out)
+    ]
+    routes = routes.reshape(heads, 1, tokens)
+    pack, attend, unpack = build_dense(tokens, features, heads, owners)
+    packed, place, counts = pack(routes, *tensors)
+    gathered = lax.all_gather(counts.reshape(heads, -1), "seq")
+    loads = jnp.sum(gathered.reshape(owners, heads, -1, OWNED), axis=3)
+    fullest = lax.all_gather(jnp.full((8, 128), jnp.max(loads)), "head")
+    overflow = jnp.max(fullest) > MESSAGE_ROWS
+    own = lax.dynamic_slice_in_dim(
+        gathered.reshape(owners, -1), lax.axis_index("seq") * OWNED, OWNED, axis=1
+    )
+    results = attend(own.reshape(owners // SOURCES, SOURCES * OWNED), exchange(packed, owners))
+    returned = exchange(results, owners)
+
+    def padded(place, returned, routes, *tensors):
+        pack, attend, unpack = build(tokens, features, heads, owners)
+        packed, place = pack(routes, *tensors)
+        return tuple(unpack(place, exchange(attend(exchange(packed, owners)), owners)))
+
+    def dense(place, returned, routes, *tensors):
+        return tuple(unpack(place, returned))
+
+    return lax.cond(overflow, padded, dense, place, returned, routes, *tensors)
 
 
 def solution(mesh):

time: 334 us -> 378 us (1.13)
  the two profiles are of different devices: /device:TPU:1 before, /device:TPU:54 now
where the time goes in v3:
time: 378 us
  blocking collectives  205 us (54%)
  waiting for transfers between devices  98.4 us (26%)
  starting transfers between devices  31.9 us (8%)
  Pallas kernels  28.2 us (7%)
  local copies, waits for them, and re-layouts  7.64 us (2%)
  other arithmetic  4.53 us (1%)
    all_gather x1, blocking collectives, body(): gathered = lax.all_gather(counts.reshape(heads, -1), 'seq')  198 us
    all_to_all x2, waiting for transfers between devices, exchange(): lax.all_to_all(packed.reshape(owners, -1, packed.shape[1]), 'seq', split_...  98.4 us
    all_to_all x2, starting transfers between devices, exchange(): lax.all_to_all(packed.reshape(owners, -1, packed.shape[1]), 'seq', split_...  31.9 us
    pallas_call x1, Pallas kernels, body(): attend(own.reshape(owners // SOURCES, SOURCES * OWNED), exchange(packed,...  20.4 us
  transfers between devices with their start and end apart: 2, of which 1 were waited for; matrix products, arithmetic and copies ran while one was open for 3% of the time, Pallas kernels for 0%

profile of v3, /device:TPU:54, one launch (start us, length us, event | category | flops | bytes accessed | tf_op | source)
XLA Modules:
  0.0 377.5 jit_solution(14587840444824076875)
XLA Ops:
  0.6 5.2 %dense_pack_rows.1 = (bf16[11264,128]{1,0:T(8,128)(2,1)S(1)}, s32[8,1,256]{2,1,0:T(1,128)S(1)}, s32[8,1,64]{2,1,0:T(1,128)S(1)}) custom-call(s32[8,1,256]{2,1,0:T(1,128)} %bitcast.20, bf16[256,1024]{1,0:T(8,128)(2,1)} %refs_1_.1, bf16[256,1024]{1,0:T(8,128)(2,1)} %refs_2_.1, bf16[256,1024]{1,0:T(8,128)(2,1)} %refs_3_.1, bf16[256,1024]{1,0:T(8,128)(2,1)} %refs_4_.1), custom_call_target="tpu_custom_call" | custom-call | tf_op jit(solution)/shard_map/dense_pack_rows/pallas_call | solution.py:376
  5.8 0.0 copy-start
  5.8 1.6 copy-done
  7.4 18.3 %all-to-all-start.2 = ((bf16[64,176,128]{2,1,0:T(8,128)(2,1)}), bf16[64,176,128]{2,1,0:T(8,128)(2,1)S(1)}, u32[]{:S(2)}, u32[]{:S(2)}) async-start(bf16[64,176,128]{2,1,0:T(8,128)(2,1)} %bitcast.18), calls=%async_computation.2 | async-start | bytes 5767168 | tf_op jit(solution)/shard_map/all_to_all | solution.py:360
  25.7 198.5 %all-gather = s32[512,1,64]{2,1,0:T(1,128)S(1)} all-gather(s32[8,1,64]{2,1,0:T(1,128)S(1)} %get-tuple-element.31), channel_id=3, replica_groups=mesh['seq'=64,'head'=8] {'seq'}, dimensions={0}, use_global_device_ids=true | all-gather | bytes 133120 | tf_op jit(solution)/shard_map/all_gather | solution.py:377
  224.2 0.5 broadcast.6
  224.8 1.3 reduce.4
  226.1 0.1 reshape.47
  226.2 0.1 constant_dynamic-slice_fusion
  226.3 0.1 reshape.48.counts_ref
  226.3 0.0 all-to-all-done.2
  226.3 20.4 %dense_cluster_attention.1 = bf16[11264,128]{1,0:T(8,128)(2,1)} custom-call(s32[16,32]{1,0:T(8,128)S(1)} %reshape.48.counts_ref, bf16[11264,128]{1,0:T(8,128)(2,1)S(1)} %bitcast.16), custom_call_target="tpu_custom_call" | custom-call | tf_op jit(solution)/shard_map/dense_cluster_attention/pallas_call | solution.py:384
  246.8 13.6 %all-to-all-start.3 = ((bf16[64,176,128]{2,1,0:T(8,128)(2,1)}), bf16[64,176,128]{2,1,0:T(8,128)(2,1)S(1)}, u32[]{:S(2)}, u32[]{:S(2)}) async-start(bf16[64,176,128]{2,1,0:T(8,128)(2,1)} %bitcast.10), calls=%async_computation.3 | async-start | bytes 5767168 | tf_op jit(solution)/shard_map/all_to_all | solution.py:360
  260.3 0.0 copy-start.1
  260.4 0.1 copy.19
  260.5 2.5 reshape.46
  263.0 1.8 reduce_sum.9
  264.8 1.3 dynamic-slice
  266.1 0.7 reduce_max.18
  266.8 1.4 dynamic-update-slice
  268.2 7.0 %all-reduce = s32[8]{0:T(128)S(1)} all-reduce(s32[8]{0:T(128)S(1)} %dynamic-update-slice), channel_id=2, replica_groups=mesh['seq'=64,'head'=8] {'head'}, use_global_device_ids=true, to_apply=%add | all-reduce | flops 8 | bytes 64
  275.2 0.7 broadcast_reduce_fusion
  276.6 98.4 %all-to-all-done.3 = bf16[64,176,128]{2,1,0:T(8,128)(2,1)S(1)} async-done(((bf16[64,176,128]{2,1,0:T(8,128)(2,1)}), bf16[64,176,128]{2,1,0:T(8,128)(2,1)S(1)}, u32[]{:S(2)}, u32[]{:S(2)}) %all-to-all-start.3) | async-done | bytes 2883616 | tf_op jit(solution)/shard_map/all_to_all | solution.py:360
  375.0 0.0 copy-done.1
  375.0 2.6 conditional.1
  375.0 2.6 dense_unpack_rows.1
  (1 shorter events, 0.0 us)
Async XLA Ops:
  5.8 1.6 copy-start
  7.4 218.9 %all-to-all-start.2 = ((bf16[64,176,128]{2,1,0:T(8,128)(2,1)}), bf16[64,176,128]{2,1,0:T(8,128)(2,1)S(1)}, u32[]{:S(2)}, u32[]{:S(2)}) async-start(bf16[64,176,128]{2,1,0:T(8,128)(2,1)} %bitcast.18), calls=%async_computation.2 | async-start | bytes 5767168 | tf_op jit(solution)/shard_map/all_to_all | solution.py:360
  246.8 128.2 %all-to-all-start.3 = ((bf16[64,176,128]{2,1,0:T(8,128)(2,1)}), bf16[64,176,128]{2,1,0:T(8,128)(2,1)S(1)}, u32[]{:S(2)}, u32[]{:S(2)}) async-start(bf16[64,176,128]{2,1,0:T(8,128)(2,1)} %bitcast.10), calls=%async_computation.3 | async-start | bytes 5767168 | tf_op jit(solution)/shard_map/all_to_all | solution.py:360
  260.3 114.6 %copy-start.1 = (s32[8,256,1]{1,2,0:T(1,128)S(1)}, s32[8,256,1]{1,2,0:T(1,128)}, u32[]{:S(2)}) copy-start(s32[8,256,1]{1,2,0:T(1,128)} %param.11) | copy-start | bytes 24580

commit v4 on v2

--- a/solution.py
+++ b/solution.py
@@ -12,6 +12,7 @@
 PACK_HEADS = 4
 ATTEND_HEADS = 2
 UNPACK_HEADS = 4
+TOKEN_HOPS = 4
 
 
 def dot_nn(left, right):
@@ -87,7 +88,7 @@
         out_ref[:, lanes] = scratch_out[j].astype(jnp.bfloat16)
 
 
-def unpack_kernel(place_ref, in_ref, o_ref, dq_ref, dk_ref, dv_ref, scratch):
+def unpack_kernel(place_ref, in_ref, token_ref, o_ref, dq_ref, dk_ref, dv_ref, scratch):
     rows = in_ref.shape[0] // 4
     group, _, tokens = place_ref.shape
     size = o_ref.shape[1] // group
@@ -149,7 +150,11 @@
     unpack = pl.pallas_call(
         unpack_kernel,
         grid=(heads // UNPACK_HEADS,),
-        in_specs=[head_row(UNPACK_HEADS), packed_block(UNPACK_HEADS)],
+        in_specs=[
+            head_row(UNPACK_HEADS),
+            packed_block(UNPACK_HEADS),
+            pl.BlockSpec(memory_space=pl.ANY),
+        ],
         out_specs=[head_rows(UNPACK_HEADS)] * 4,
         out_shape=[jax.ShapeDtypeStruct((tokens, features), jnp.bfloat16)] * 4,
         scratch_shapes=[scratch(UNPACK_HEADS)],
@@ -181,8 +186,18 @@
         in_hbm(values),
         in_hbm(grad_out),
     )
+    token = place[:, 0, :128]
+    groups = lax.axis_size("head")
+    turns = [
+        (s * groups + h, (s + owners // 2 + 8) % owners * groups + h)
+        for s in range(owners)
+        for h in range(1, groups, 2)
+    ]
+    for _ in range(TOKEN_HOPS):
+        token = jnp.maximum(token, lax.ppermute(token, ("seq", "head"), turns))
+    packed, token = lax.optimization_barrier((packed, token))
     results = attend(exchange(packed))
-    return tuple(unpack(place, exchange(results)))
+    return tuple(unpack(place, exchange(results), token))
 
 
 def solution(mesh):

time: 334 us -> 313 us (0.937)
  blocking collectives: 310 us -> 222 us
  starting transfers between devices: 0 us -> 66.3 us
    all_to_all x2, blocking collectives: 310 us -> 222 us  [exchange(): lax.all_to_all(packed.reshape(owners, -1, features), 'seq', split_axis=0,...]
    ppermute x0 -> x4, starting transfers between devices: none -> 66.3 us  [body(): token = jnp.maximum(token, lax.ppermute(token, ('seq', 'head'), turns))]
  transfers between devices with their start and end apart: 0 -> 4, of which waited for: 0 -> 4; matrix products, arithmetic and copies ran while one was open for 0% -> 0% of each run, Pallas kernels for 0% -> 0%
where the time goes in v4:
time: 313 us
  blocking collectives  222 us (71%)
  starting transfers between devices  66.3 us (21%)
  Pallas kernels  19.6 us (6%)
    all_to_all x2, blocking collectives, exchange(): lax.all_to_all(packed.reshape(owners, -1, features), 'seq', split_axis=0,...  222 us
    ppermute x4, starting transfers between devices, body(): token = jnp.maximum(token, lax.ppermute(token, ('seq', 'head'), turns))  66.3 us
    pallas_call x1, Pallas kernels, body(): results = attend(exchange(packed))  10.2 us
  transfers between devices with their start and end apart: 4, of which 4 were waited for; matrix products, arithmetic and copies ran while one was open for 0% of the time, Pallas kernels for 0%

profile of v4, /device:TPU:1, one launch (start us, length us, event | category | flops | bytes accessed | tf_op | source)
XLA Modules:
  0.0 312.6 jit_solution(18333110842238375738)
XLA Ops:
  0.6 5.4 %pack_rows.1 = (bf16[1536,1024]{1,0:T(8,128)(2,1)}, s32[8,1,256]{2,1,0:T(1,128)}) custom-call(s32[8,1,256]{2,1,0:T(1,128)} %bitcast.13, bf16[256,1024]{1,0:T(8,128)(2,1)} %refs_1_.1, bf16[256,1024]{1,0:T(8,128)(2,1)} %refs_2_.1, bf16[256,1024]{1,0:T(8,128)(2,1)} %refs_3_.1, bf16[256,1024]{1,0:T(8,128)(2,1)} %refs_4_.1), custom_call_target="tpu_custom_call" | custom-call | tf_op jit(solution)/shard_map/pack_rows/pallas_call | solution.py:182
  6.1 0.7 copy.9
  6.8 18.7 %collective-permute-start = (s32[8,128]{1,0:T(8,128)S(1)}, s32[8,128]{1,0:T(8,128)S(1)}, u32[]{:S(2)}, u32[]{:S(2)}) collective-permute-start(s32[8,128]{1,0:T(8,128)S(1)} %slice_bitcast_fusion), channel_id=1, source_target_pairs={{1,321},{3,323},{5,325},{7,327},{9,329},{11,331},{13,333},{15,335}... | collective-permute-start | bytes 12296 | tf_op jit(solution)/shard_map/ppermute | solution.py:197
  25.5 0.7 collective-permute-done
  26.2 14.7 %collective-permute-start.1 = (s32[8,128]{1,0:T(8,128)S(1)}, s32[8,128]{1,0:T(8,128)S(1)}, u32[]{:S(2)}, u32[]{:S(2)}) collective-permute-start(s32[8,128]{1,0:T(8,128)S(1)} %fusion), channel_id=1, source_target_pairs={{1,321},{3,323},{5,325},{7,327},{9,329},{11,331},{13,333},{15,335}... | collective-permute-start | bytes 12296 | tf_op jit(solution)/shard_map/ppermute | solution.py:197
  41.0 0.7 collective-permute-done.1
  41.7 16.8 %collective-permute-start.2 = (s32[8,128]{1,0:T(8,128)S(1)}, s32[8,128]{1,0:T(8,128)S(1)}, u32[]{:S(2)}, u32[]{:S(2)}) collective-permute-start(s32[8,128]{1,0:T(8,128)S(1)} %max.13), channel_id=1, source_target_pairs={{1,321},{3,323},{5,325},{7,327},{9,329},{11,331},{13,333},{15,335}... | collective-permute-start | bytes 12296 | tf_op jit(solution)/shard_map/ppermute | solution.py:197
  58.5 0.7 collective-permute-done.2
  59.3 16.1 %collective-permute-start.3 = (s32[8,128]{1,0:T(8,128)S(1)}, s32[8,128]{1,0:T(8,128)S(1)}, u32[]{:S(2)}, u32[]{:S(2)}) collective-permute-start(s32[8,128]{1,0:T(8,128)S(1)} %max.14), channel_id=1, source_target_pairs={{1,321},{3,323},{5,325},{7,327},{9,329},{11,331},{13,333},{15,335}... | collective-permute-start | bytes 12296 | tf_op jit(solution)/shard_map/ppermute | solution.py:197
  75.4 0.7 collective-permute-done.3
  76.1 0.6 max.15.token_ref
  76.7 127.1 %all_to_all.10 = bf16[64,24,1024]{2,1,0:T(8,128)(2,1)} all-to-all(bf16[64,24,1024]{2,1,0:T(8,128)(2,1)} %bitcast.12), channel_id=1, replica_groups=mesh['seq'=64,'head'=8] {'seq'}, dimensions={0} | all-to-all | bytes 6291456 | tf_op jit(solution)/shard_map/all_to_all | solution.py:174
  203.8 10.2 %cluster_attention.1 = bf16[1536,1024]{1,0:T(8,128)(2,1)} custom-call(bf16[1536,1024]{1,0:T(8,128)(2,1)} %bitcast.10), custom_call_target="tpu_custom_call" | custom-call | tf_op jit(solution)/shard_map/cluster_attention/pallas_call | solution.py:199
  214.0 94.6 %all_to_all.11 = bf16[64,24,1024]{2,1,0:T(8,128)(2,1)} all-to-all(bf16[64,24,1024]{2,1,0:T(8,128)(2,1)} %bitcast.11), channel_id=1, replica_groups=mesh['seq'=64,'head'=8] {'seq'}, dimensions={0} | all-to-all | bytes 6291456 | tf_op jit(solution)/shard_map/all_to_all | solution.py:174
  308.7 4.0 %unpack_rows.1 = (bf16[256,1024]{1,0:T(8,128)(2,1)}, bf16[256,1024]{1,0:T(8,128)(2,1)}, bf16[256,1024]{1,0:T(8,128)(2,1)}, bf16[256,1024]{1,0:T(8,128)(2,1)}) custom-call(s32[8,1,256]{2,1,0:T(1,128)} %get-tuple-element.8.place_ref, bf16[1536,1024]{1,0:T(8,128)(2,1)} %bitcast.9, s32[8,128]{1,0:T(8,128)} %max.15.token_ref), custom_call_target="tpu_custom_call" | custom-call | tf_op jit(solution)/shard_map/unpack_rows/pallas_call | solution.py:200
  (4 shorter events, 0.0 us)
Async XLA Ops:
  6.8 19.5 %collective-permute-start = (s32[8,128]{1,0:T(8,128)S(1)}, s32[8,128]{1,0:T(8,128)S(1)}, u32[]{:S(2)}, u32[]{:S(2)}) collective-permute-start(s32[8,128]{1,0:T(8,128)S(1)} %slice_bitcast_fusion), channel_id=1, source_target_pairs={{1,321},{3,323},{5,325},{7,327},{9,329},{11,331},{13,333},{15,335}... | collective-permute-start | bytes 12296 | tf_op jit(solution)/shard_map/ppermute | solution.py:197
  26.2 15.5 %collective-permute-start.1 = (s32[8,128]{1,0:T(8,128)S(1)}, s32[8,128]{1,0:T(8,128)S(1)}, u32[]{:S(2)}, u32[]{:S(2)}) collective-permute-start(s32[8,128]{1,0:T(8,128)S(1)} %fusion), channel_id=1, source_target_pairs={{1,321},{3,323},{5,325},{7,327},{9,329},{11,331},{13,333},{15,335}... | collective-permute-start | bytes 12296 | tf_op jit(solution)/shard_map/ppermute | solution.py:197
  41.7 17.5 %collective-permute-start.2 = (s32[8,128]{1,0:T(8,128)S(1)}, s32[8,128]{1,0:T(8,128)S(1)}, u32[]{:S(2)}, u32[]{:S(2)}) collective-permute-start(s32[8,128]{1,0:T(8,128)S(1)} %max.13), channel_id=1, source_target_pairs={{1,321},{3,323},{5,325},{7,327},{9,329},{11,331},{13,333},{15,335}... | collective-permute-start | bytes 12296 | tf_op jit(solution)/shard_map/ppermute | solution.py:197
  59.3 16.8 %collective-permute-start.3 = (s32[8,128]{1,0:T(8,128)S(1)}, s32[8,128]{1,0:T(8,128)S(1)}, u32[]{:S(2)}, u32[]{:S(2)}) collective-permute-start(s32[8,128]{1,0:T(8,128)S(1)} %max.14), channel_id=1, source_target_pairs={{1,321},{3,323},{5,325},{7,327},{9,329},{11,331},{13,333},{15,335}... | collective-permute-start | bytes 12296 | tf_op jit(solution)/shard_map/ppermute | solution.py:197

commit v5 on v3

--- a/solution.py
+++ b/solution.py
@@ -16,6 +16,7 @@
 PACK_HEADS = 4
 ATTEND_HEADS = 2
 UNPACK_HEADS = 4
+TOKEN_HOPS = 3
 
 
 def dot_nn(left, right):
@@ -59,13 +60,11 @@
         out_ref[:, lanes] = scratch[j].astype(jnp.bfloat16)
 
 
-def attend_cluster(query, key, value, grad):
+def attend_cluster(query, key, value, grad, keep):
     size = query.shape[1]
     scaling = 1.0 / math.sqrt(size)
-    first_lane = jnp.where(lax.broadcasted_iota(jnp.int32, (8, size), 1) == 0, 1.0, 0.0)
-    marks = dot_nt(first_lane.astype(jnp.bfloat16), key)[0:1]
     scores = dot_nt(query, key) * scaling
-    masked = jnp.where(marks < DEAD_TEST, scores, -1e30)
+    masked = jnp.where(keep, scores, -1e30)
     weights = jnp.exp(masked - jnp.max(masked, axis=1, keepdims=True))
     probability = weights * (1.0 / jnp.sum(weights, axis=1, keepdims=True))
     probability_low = probability.astype(jnp.bfloat16)
@@ -89,7 +88,9 @@
         lanes = slice(j * size, (j + 1) * size)
         scratch[j] = in_ref[:, lanes].astype(jnp.float32)
         tensors = [scratch[j, pl.ds(i, rows, stride=4), :].astype(jnp.bfloat16) for i in range(4)]
-        for i, result in enumerate(attend_cluster(*tensors)):
+        first_lane = jnp.where(lax.broadcasted_iota(jnp.int32, (8, size), 1) == 0, 1.0, 0.0)
+        keep = dot_nt(first_lane.astype(jnp.bfloat16), tensors[1])[0:1] < DEAD_TEST
+        for i, result in enumerate(attend_cluster(*tensors, keep)):
             scratch_out[j, pl.ds(i, rows, stride=4), :] = result
         out_ref[:, lanes] = scratch_out[j].astype(jnp.bfloat16)
 
@@ -113,11 +114,12 @@
 
 
 def dense_pack_kernel(
-    routes_ref, q_ref, k_ref, v_ref, g_ref, out_ref, place_ref, counts_ref, scratch, *, clusters
+    routes_ref, q_ref, k_ref, v_ref, g_ref, out_ref, place_ref, scratch, *, clusters
 ):
     group, _, tokens = routes_ref.shape
     rows = scratch.shape[1] // 4
     size = q_ref.shape[1] // group
+    octets = clusters // OWNED
     earlier = lax.broadcasted_iota(jnp.int32, (tokens, tokens), 0) < lax.broadcasted_iota(
         jnp.int32, (tokens, tokens), 1
     )
@@ -129,16 +131,24 @@
     all_tokens = jnp.ones((tokens, tokens), jnp.bfloat16)
     cluster_ids = lax.broadcasted_iota(jnp.int32, (clusters, tokens), 0)
     row_ids = lax.broadcasted_iota(jnp.int32, (rows, tokens), 0)
+    in_octet = lax.broadcasted_iota(jnp.int32, (octets, clusters), 1) // OWNED == (
+        lax.broadcasted_iota(jnp.int32, (octets, clusters), 0)
+    )
+    to_lane = lax.broadcasted_iota(jnp.int32, (clusters, size), 0) % OWNED == (
+        lax.broadcasted_iota(jnp.int32, (clusters, size), 1)
+    )
+    to_lane_low = jnp.where(to_lane, 1.0, 0.0).astype(jnp.bfloat16)
     for j in range(group):
         lanes = slice(j * size, (j + 1) * size)
         route = routes_ref[j]
         onehot = cluster_ids == route
         onehot_low = jnp.where(onehot, 1.0, 0.0).astype(jnp.bfloat16)
-        counts_ref[j] = dot_nt(all_tokens[:8], onehot_low)[0:1].astype(jnp.int32)
+        counts = dot_nt(all_tokens[:octets], onehot_low)
+        counts = jnp.where(in_octet, counts, 0.0)
         in_lower = dot_nn(lower_low, onehot_low).astype(jnp.bfloat16)
         before = dot_nn(onehot_low, earlier_low) + dot_nn(in_lower, all_tokens)
         ranking = jnp.sum(jnp.where(onehot, before, 0.0), axis=0, keepdims=True)
-        place = route // OWNED * MESSAGE_ROWS + ranking.astype(jnp.int32)
+        place = route // OWNED * MESSAGE_ROWS + 1 + ranking.astype(jnp.int32)
         place_ref[j] = place
         select = jnp.where(row_ids == place, 1.0, 0.0).astype(jnp.bfloat16)
         query_key = dot_nn(select, jnp.concatenate([q_ref[:, lanes], k_ref[:, lanes]], axis=1))
@@ -147,32 +157,60 @@
         scratch[j, pl.ds(1, rows, stride=4), :] = query_key[:, size:]
         scratch[j, pl.ds(2, rows, stride=4), :] = value_grad[:, :size]
         scratch[j, pl.ds(3, rows, stride=4), :] = value_grad[:, size:]
+        scratch[j, pl.ds(0, octets, stride=4 * MESSAGE_ROWS), :] = dot_nn(
+            counts.astype(jnp.bfloat16), to_lane_low
+        )
         out_ref[j * 4 * rows : (j + 1) * 4 * rows, :] = scratch[j].astype(jnp.bfloat16)
 
 
-def dense_attention_kernel(counts_ref, in_ref, out_ref, target_ref, stage, wide_ref):
+def dense_attention_kernel(
+    in_ref, token_ref, out_ref, target_ref, stage, wide_ref, *, slots
+):
     size = in_ref.shape[1]
-    steps, pairs = counts_ref.shape
     count = SOURCES * MESSAGE_ROWS
-    wide = pairs * WIDE
-    sources = steps * SOURCES
-    slots = wide_ref.shape[1] // (sources * OWNED) - 2
-    lanes = lax.broadcasted_iota(jnp.int32, (pairs, wide), 1) // WIDE
-    pair = lax.broadcasted_iota(jnp.int32, (pairs, wide), 0)
-    counts_low = counts_ref[...].astype(jnp.bfloat16)
-    same = jnp.where(lanes == pair, 1.0, 0.0).astype(jnp.bfloat16)
-    ahead = jnp.logical_and(pair < lanes, pair // OWNED == lanes // OWNED)
-    ahead = jnp.where(ahead, 1.0, 0.0).astype(jnp.bfloat16)
-    lane = lax.broadcasted_iota(jnp.int32, (steps, wide), 1)
+    wide = SOURCES * OWNED * WIDE
+    sources = in_ref.shape[0] // (4 * MESSAGE_ROWS)
+    steps = sources // SOURCES
+    for s in range(sources):
+        head_rows = in_ref[s * 4 * MESSAGE_ROWS : s * 4 * MESSAGE_ROWS + 16, :]
+        stage[0, s : s + 1, :] = head_rows.astype(jnp.float32)[0:1]
+    counts = stage[0, 0:sources, :]
+    counts_low = counts.astype(jnp.bfloat16)
+    most = jnp.max(jnp.sum(counts, axis=1, keepdims=True), axis=0, keepdims=True)
+    overflow = jnp.broadcast_to(jnp.where(most > MESSAGE_ROWS - 1, 1.0, 0.0), (SOURCES, size))
+    lane = lax.broadcasted_iota(jnp.int32, (size, wide), 1)
+    lane_cluster = lane // WIDE % OWNED
+    cluster = lax.broadcasted_iota(jnp.int32, (size, wide), 0)
+    same = jnp.where(lane_cluster == cluster, 1.0, 0.0).astype(jnp.bfloat16)
+    ahead = jnp.where(cluster < lane_cluster, 1.0, 0.0).astype(jnp.bfloat16)
+    lane = lax.broadcasted_iota(jnp.int32, (sources, wide), 1)
+    source = lax.broadcasted_iota(jnp.int32, (sources, wide), 0)
     slot = lane % WIDE
-    target = dot_nn(counts_low, ahead).astype(jnp.int32) + slot
-    target = target + lane // (OWNED * WIDE) * MESSAGE_ROWS
-    target_ref[...] = jnp.where(slot < dot_nn(counts_low, same).astype(jnp.int32), target, -1)
+    spread = dot_nn(counts_low, same).astype(jnp.int32)
+    target = dot_nn(counts_low, ahead).astype(jnp.int32) + slot + 1 + source % SOURCES * MESSAGE_ROWS
+    live = jnp.logical_and(slot < spread, lane // (OWNED * WIDE) == source % SOURCES)
+    steps_of = lax.broadcasted_iota(jnp.int32, (steps, sources), 1) // SOURCES == (
+        lax.broadcasted_iota(jnp.int32, (steps, sources), 0)
+    )
+    target_ref[...] = dot_nn(
+        jnp.where(steps_of, 1.0, 0.0).astype(jnp.bfloat16),
+        jnp.where(live, target, 0).astype(jnp.float32).astype(jnp.bfloat16),
+    ).astype(jnp.int32)
+    slot_lane = lax.broadcasted_iota(jnp.int32, (sources, slots * sources), 1)
+    repeat = lax.broadcasted_iota(jnp.int32, (sources, slots * sources), 0) == slot_lane % sources
+    repeated = lax.dot_general(
+        counts_low,
+        jnp.where(repeat, 1.0, 0.0).astype(jnp.bfloat16),
+        (((0,), (0,)), ((), ())),
+        preferred_element_type=jnp.float32,
+    )[:OWNED].astype(jnp.int32)
+    keep = repeated > lax.broadcasted_iota(jnp.int32, (OWNED, slots * sources), 1) // sources
     row_ids = lax.broadcasted_iota(jnp.int32, (count, wide), 0)
-    ones = jnp.ones((count, size), jnp.bfloat16)
 
     def selection(step):
-        return jnp.where(row_ids == target_ref[pl.ds(step, 1), :], 1.0, 0.0).astype(jnp.bfloat16)
+        target = target_ref[pl.ds(step, 1), :]
+        select = jnp.logical_and(row_ids == target, target > 0)
+        return jnp.where(select, 1.0, 0.0).astype(jnp.bfloat16)
 
     def expand(pass_id, carry):
         for u in range(stage.shape[0]):
@@ -183,9 +221,8 @@
             into = pl.ds(step * wide, wide)
             query_key = dot_tn(select, jnp.concatenate(parts[:2], axis=1))
             value_grad = dot_tn(select, jnp.concatenate(parts[2:], axis=1))
-            live = dot_tn(select, ones)
             wide_ref[0, into, :] = query_key[:, :size]
-            wide_ref[1, into, :] = query_key[:, size:] + (1.0 - live) * DEAD_KEY
+            wide_ref[1, into, :] = query_key[:, size:]
             wide_ref[2, into, :] = value_grad[:, :size]
             wide_ref[3, into, :] = value_grad[:, size:]
         return carry
@@ -203,6 +240,7 @@
             stage[u, pl.ds(1, count, stride=4), :] = first[:, size:]
             stage[u, pl.ds(2, count, stride=4), :] = second[:, :size]
             stage[u, pl.ds(3, count, stride=4), :] = second[:, size:]
+            stage[u, pl.ds(0, SOURCES, stride=4 * MESSAGE_ROWS), :] = overflow
             out_ref[pl.ds(step * 4 * count, 4 * count), :] = stage[u].astype(jnp.bfloat16)
         return carry
 
@@ -213,7 +251,7 @@
             jnp.concatenate([wide_ref[i, spot, :] for spot in spots], axis=0).astype(jnp.bfloat16)
             for i in range(4)
         ]
-        for i, result in enumerate(attend_cluster(*tensors)):
+        for i, result in enumerate(attend_cluster(*tensors, keep[c : c + 1])):
             for s, spot in enumerate(spots):
                 wide_ref[i, spot, :] = result[s * sources : (s + 1) * sources]
     lax.fori_loop(0, steps // stage.shape[0], compact, 0)
@@ -296,9 +334,8 @@
     clusters = heads * OWNED
     rows = OWNED * MESSAGE_ROWS
     slots = 3 * tokens // (2 * owners)
-    steps = owners // SOURCES
     params = pltpu.CompilerParams(
-        dimension_semantics=("arbitrary",), vmem_limit_bytes=40 * 1024 * 1024
+        dimension_semantics=("arbitrary",), vmem_limit_bytes=60 * 1024 * 1024
     )
     packed_shape = jax.ShapeDtypeStruct((heads * 4 * rows, size), jnp.bfloat16)
 
@@ -321,22 +358,21 @@
         out_specs=[
             packed_block(PACK_HEADS),
             head_row(PACK_HEADS, tokens),
-            head_row(PACK_HEADS, clusters),
         ],
         out_shape=[
             packed_shape,
             jax.ShapeDtypeStruct((heads, 1, tokens), jnp.int32),
-            jax.ShapeDtypeStruct((heads, 1, clusters), jnp.int32),
         ],
         scratch_shapes=[scratch(PACK_HEADS)],
         compiler_params=params,
         name="dense_pack_rows",
     )
     attend = pl.pallas_call(
-        dense_attention_kernel,
+        lambda *refs: dense_attention_kernel(*refs, slots=slots),
+        in_specs=[pl.BlockSpec(memory_space=pltpu.VMEM), pl.BlockSpec(memory_space=pl.ANY)],
         out_shape=packed_shape,
         scratch_shapes=[
-            pltpu.VMEM((steps, SOURCES * OWNED * WIDE), jnp.int32),
+            pltpu.VMEM((owners // SOURCES, SOURCES * OWNED * WIDE), jnp.int32),
             pltpu.VMEM((2, 4 * SOURCES * MESSAGE_ROWS, size), jnp.float32),
             pltpu.VMEM((4, owners * OWNED * WIDE, size), jnp.float32),
         ],
@@ -373,16 +409,19 @@
     ]
     routes = routes.reshape(heads, 1, tokens)
     pack, attend, unpack = build_dense(tokens, features, heads, owners)
-    packed, place, counts = pack(routes, *tensors)
-    gathered = lax.all_gather(counts.reshape(heads, -1), "seq")
-    loads = jnp.sum(gathered.reshape(owners, heads, -1, OWNED), axis=3)
-    fullest = lax.all_gather(jnp.full((8, 128), jnp.max(loads)), "head")
-    overflow = jnp.max(fullest) > MESSAGE_ROWS
-    own = lax.dynamic_slice_in_dim(
-        gathered.reshape(owners, -1), lax.axis_index("seq") * OWNED, OWNED, axis=1
-    )
-    results = attend(own.reshape(owners // SOURCES, SOURCES * OWNED), exchange(packed, owners))
-    returned = exchange(results, owners)
+    packed, place = pack(routes, *tensors)
+    token = place[:, 0, :128]
+    groups = lax.axis_size("head")
+    turns = [
+        (s * groups + h, (s + owners // 2 + 8) % owners * groups + h)
+        for s in range(owners)
+        for h in range(1, groups, 2)
+    ]
+    for _ in range(TOKEN_HOPS):
+        token = jnp.maximum(token, lax.ppermute(token, ("seq", "head"), turns))
+    packed, token = lax.optimization_barrier((packed, token))
+    returned = exchange(attend(exchange(packed, owners), token), owners)
+    overflow = jnp.max(returned.reshape(owners, -1, returned.shape[1])[:, 0, 0]) > 0.5
 
     def padded(place, returned, routes, *tensors):
         pack, attend, unpack = build(tokens, features, heads, owners)

time: 378 us -> 290 us (0.77)
  the two profiles are of different devices: /device:TPU:54 before, /device:TPU:1 now
where the time goes in v5:
time: 290 us; the launch traced here: 289 us
  blocking collectives  108 us (37%)
  waiting for transfers between devices  91.2 us (31%)
  starting transfers between devices  59.6 us (21%)
  Pallas kernels  28.7 us (10%)
    all_to_all x1, blocking collectives, exchange(): lax.all_to_all(packed.reshape(owners, -1, packed.shape[1]), 'seq', split_...  108 us
    all_to_all x1, waiting for transfers between devices, exchange(): lax.all_to_all(packed.reshape(owners, -1, packed.shape[1]), 'seq', split_...  88 us
    ppermute x3, starting transfers between devices, body(): token = jnp.maximum(token, lax.ppermute(token, ('seq', 'head'), turns))  49.1 us
    pallas_call x1, Pallas kernels, body(): returned = exchange(attend(exchange(packed, owners), token), owners)  20 us
    all_to_all x1, starting transfers between devices, exchange(): lax.all_to_all(packed.reshape(owners, -1, packed.shape[1]), 'seq', split_...  10.5 us
    pallas_call x1, Pallas kernels, body(): packed, place = pack(routes, *tensors)  6.2 us
  transfers between devices with their start and end apart: 4, of which 4 were waited for; matrix products, arithmetic and copies ran while one was open for 0% of the time, Pallas kernels for 0%

profile of v5, /device:TPU:1, one launch (start us, length us, event | category | flops | bytes accessed | tf_op | source)
XLA Modules:
  0.0 289.2 jit_solution(10658748770048612007)
XLA Ops:
  0.6 6.2 %dense_pack_rows.1 = (bf16[11264,128]{1,0:T(8,128)(2,1)}, s32[8,1,256]{2,1,0:T(1,128)S(1)}) custom-call(s32[8,1,256]{2,1,0:T(1,128)} %bitcast.20, bf16[256,1024]{1,0:T(8,128)(2,1)} %refs_1_.1, bf16[256,1024]{1,0:T(8,128)(2,1)} %refs_2_.1, bf16[256,1024]{1,0:T(8,128)(2,1)} %refs_3_.1, bf16[256,1024]{1,0:T(8,128)(2,1)} %refs_4_.1), custom_call_target="tpu_custom_call" | custom-call | tf_op jit(solution)/shard_map/dense_pack_rows/pallas_call | solution.py:412
  6.8 18.7 %collective-permute-start = (s32[8,128]{1,0:T(8,128)S(1)}, s32[8,128]{1,0:T(8,128)S(1)}, u32[]{:S(2)}, u32[]{:S(2)}) collective-permute-start(s32[8,128]{1,0:T(8,128)S(1)} %slice_bitcast_fusion), channel_id=1, source_target_pairs={{1,321},{3,323},{5,325},{7,327},{9,329},{11,331},{13,333},{15,335}... | collective-permute-start | bytes 12296 | tf_op jit(solution)/shard_map/ppermute | solution.py:421
  25.6 0.7 collective-permute-done
  26.3 14.7 %collective-permute-start.1 = (s32[8,128]{1,0:T(8,128)S(1)}, s32[8,128]{1,0:T(8,128)S(1)}, u32[]{:S(2)}, u32[]{:S(2)}) collective-permute-start(s32[8,128]{1,0:T(8,128)S(1)} %fusion), channel_id=1, source_target_pairs={{1,321},{3,323},{5,325},{7,327},{9,329},{11,331},{13,333},{15,335}... | collective-permute-start | bytes 12296 | tf_op jit(solution)/shard_map/ppermute | solution.py:421
  41.0 0.7 collective-permute-done.1
  41.8 15.7 %collective-permute-start.2 = (s32[8,128]{1,0:T(8,128)S(1)}, s32[8,128]{1,0:T(8,128)S(1)}, u32[]{:S(2)}, u32[]{:S(2)}) collective-permute-start(s32[8,128]{1,0:T(8,128)S(1)} %max.10), channel_id=1, source_target_pairs={{1,321},{3,323},{5,325},{7,327},{9,329},{11,331},{13,333},{15,335}... | collective-permute-start | bytes 12296 | tf_op jit(solution)/shard_map/ppermute | solution.py:421
  57.4 1.7 collective-permute-done.2
  59.2 107.6 %all_to_all.20 = bf16[64,176,128]{2,1,0:T(8,128)(2,1)S(1)} all-to-all(bf16[64,176,128]{2,1,0:T(8,128)(2,1)} %bitcast.19), channel_id=1, replica_groups=mesh['seq'=64,'head'=8] {'seq'}, dimensions={0} | all-to-all | bytes 5767168 | tf_op jit(solution)/shard_map/all_to_all | solution.py:396
  166.8 20.0 %dense_cluster_attention.1 = bf16[11264,128]{1,0:T(8,128)(2,1)} custom-call(bf16[11264,128]{1,0:T(8,128)(2,1)S(1)} %bitcast.16, s32[8,128]{1,0:T(8,128)S(1)} %max.11.refs_1_), custom_call_target="tpu_custom_call" | custom-call | tf_op jit(solution)/shard_map/dense_cluster_attention/pallas_call | solution.py:423
  186.7 0.0 copy-start
  186.7 10.5 %all-to-all-start.3 = ((bf16[64,176,128]{2,1,0:T(8,128)(2,1)}), bf16[64,176,128]{2,1,0:T(8,128)(2,1)S(1)}, u32[]{:S(2)}, u32[]{:S(2)}) async-start(bf16[64,176,128]{2,1,0:T(8,128)(2,1)} %bitcast.9), calls=%async_computation.3 | async-start | bytes 5767168 | tf_op jit(solution)/shard_map/all_to_all | solution.py:396
  197.2 88.0 %all-to-all-done.3 = bf16[64,176,128]{2,1,0:T(8,128)(2,1)S(1)} async-done(((bf16[64,176,128]{2,1,0:T(8,128)(2,1)}), bf16[64,176,128]{2,1,0:T(8,128)(2,1)S(1)}, u32[]{:S(2)}, u32[]{:S(2)}) %all-to-all-start.3) | async-done | bytes 2883616 | tf_op jit(solution)/shard_map/all_to_all | solution.py:396
  285.3 0.7 slice_reduce_fusion
  286.6 0.0 copy-done
  286.6 2.6 conditional.1
  286.6 2.6 dense_unpack_rows.1
  (5 shorter events, 0.0 us)
Async XLA Ops:
  6.8 19.5 %collective-permute-start = (s32[8,128]{1,0:T(8,128)S(1)}, s32[8,128]{1,0:T(8,128)S(1)}, u32[]{:S(2)}, u32[]{:S(2)}) collective-permute-start(s32[8,128]{1,0:T(8,128)S(1)} %slice_bitcast_fusion), channel_id=1, source_target_pairs={{1,321},{3,323},{5,325},{7,327},{9,329},{11,331},{13,333},{15,335}... | collective-permute-start | bytes 12296 | tf_op jit(solution)/shard_map/ppermute | solution.py:421
  26.3 15.5 %collective-permute-start.1 = (s32[8,128]{1,0:T(8,128)S(1)}, s32[8,128]{1,0:T(8,128)S(1)}, u32[]{:S(2)}, u32[]{:S(2)}) collective-permute-start(s32[8,128]{1,0:T(8,128)S(1)} %fusion), channel_id=1, source_target_pairs={{1,321},{3,323},{5,325},{7,327},{9,329},{11,331},{13,333},{15,335}... | collective-permute-start | bytes 12296 | tf_op jit(solution)/shard_map/ppermute | solution.py:421
  41.8 17.4 %collective-permute-start.2 = (s32[8,128]{1,0:T(8,128)S(1)}, s32[8,128]{1,0:T(8,128)S(1)}, u32[]{:S(2)}, u32[]{:S(2)}) collective-permute-start(s32[8,128]{1,0:T(8,128)S(1)} %max.10), channel_id=1, source_target_pairs={{1,321},{3,323},{5,325},{7,327},{9,329},{11,331},{13,333},{15,335}... | collective-permute-start | bytes 12296 | tf_op jit(solution)/shard_map/ppermute | solution.py:421
  186.7 99.9 %copy-start = (s32[8,256,1]{1,2,0:T(1,128)S(1)}, s32[8,256,1]{1,2,0:T(1,128)}, u32[]{:S(2)}) copy-start(s32[8,256,1]{1,2,0:T(1,128)} %param.11) | copy-start | bytes 24580
  186.7 98.5 %all-to-all-start.3 = ((bf16[64,176,128]{2,1,0:T(8,128)(2,1)}), bf16[64,176,128]{2,1,0:T(8,128)(2,1)S(1)}, u32[]{:S(2)}, u32[]{:S(2)}) async-start(bf16[64,176,128]{2,1,0:T(8,128)(2,1)} %bitcast.9), calls=%async_computation.3 | async-start | bytes 5767168 | tf_op jit(solution)/shard_map/all_to_all | solution.py:396

commit v6 on v5

--- a/solution.py
+++ b/solution.py
@@ -16,7 +16,7 @@
 PACK_HEADS = 4
 ATTEND_HEADS = 2
 UNPACK_HEADS = 4
-TOKEN_HOPS = 3
+TOKEN_HOPS = 2
 
 
 def dot_nn(left, right):

time: 290 us -> 297 us (1.024)
  starting transfers between devices: 59.6 us -> 41 us
  waiting for transfers between devices: 91.2 us -> 106 us
  blocking collectives: 108 us -> 119 us
    all_to_all x1, waiting for transfers between devices: 88 us -> 104 us  [exchange(): lax.all_to_all(packed.reshape(owners, -1, packed.shape[1]), 'seq', split_...]
    ppermute x3 -> x2, starting transfers between devices: 49.1 us -> 33.4 us  [body(): token = jnp.maximum(token, lax.ppermute(token, ('seq', 'head'), turns))]
    all_to_all x1, blocking collectives: 108 us -> 119 us  [exchange(): lax.all_to_all(packed.reshape(owners, -1, packed.shape[1]), 'seq', split_...]
  transfers between devices with their start and end apart: 4 -> 3, of which waited for: 4 -> 3; matrix products, arithmetic and copies ran while one was open for 0% -> 0% of each run, Pallas kernels for 0% -> 0%
where the time goes in v6:
time: 297 us
  blocking collectives  119 us (40%)
  waiting for transfers between devices  106 us (36%)
  starting transfers between devices  41 us (14%)
  Pallas kernels  28.7 us (10%)
    all_to_all x1, blocking collectives, exchange(): lax.all_to_all(packed.reshape(owners, -1, packed.shape[1]), 'seq', split_...  119 us
    all_to_all x1, waiting for transfers between devices, exchange(): lax.all_to_all(packed.reshape(owners, -1, packed.shape[1]), 'seq', split_...  104 us
    ppermute x2, starting transfers between devices, body(): token = jnp.maximum(token, lax.ppermute(token, ('seq', 'head'), turns))  33.4 us
    pallas_call x1, Pallas kernels, body(): returned = exchange(attend(exchange(packed, owners), token), owners)  19.9 us
    all_to_all x1, starting transfers between devices, exchange(): lax.all_to_all(packed.reshape(owners, -1, packed.shape[1]), 'seq', split_...  7.58 us
    pallas_call x1, Pallas kernels, body(): packed, place = pack(routes, *tensors)  6.18 us
  transfers between devices with their start and end apart: 3, of which 3 were waited for; matrix products, arithmetic and copies ran while one was open for 0% of the time, Pallas kernels for 0%

profile of v6, /device:TPU:1, one launch (start us, length us, event | category | flops | bytes accessed | tf_op | source)
XLA Modules:
  0.0 296.7 jit_solution(12081384940090638779)
XLA Ops:
  0.6 6.2 %dense_pack_rows.1 = (bf16[11264,128]{1,0:T(8,128)(2,1)}, s32[8,1,256]{2,1,0:T(1,128)S(1)}) custom-call(s32[8,1,256]{2,1,0:T(1,128)} %bitcast.20, bf16[256,1024]{1,0:T(8,128)(2,1)} %refs_1_.1, bf16[256,1024]{1,0:T(8,128)(2,1)} %refs_2_.1, bf16[256,1024]{1,0:T(8,128)(2,1)} %refs_3_.1, bf16[256,1024]{1,0:T(8,128)(2,1)} %refs_4_.1), custom_call_target="tpu_custom_call" | custom-call | tf_op jit(solution)/shard_map/dense_pack_rows/pallas_call | solution.py:412
  6.8 18.7 %collective-permute-start = (s32[8,128]{1,0:T(8,128)S(1)}, s32[8,128]{1,0:T(8,128)S(1)}, u32[]{:S(2)}, u32[]{:S(2)}) collective-permute-start(s32[8,128]{1,0:T(8,128)S(1)} %slice_bitcast_fusion), channel_id=1, source_target_pairs={{1,321},{3,323},{5,325},{7,327},{9,329},{11,331},{13,333},{15,335}... | collective-permute-start | bytes 12296 | tf_op jit(solution)/shard_map/ppermute | solution.py:421
  25.5 0.7 collective-permute-done
  26.3 14.7 %collective-permute-start.1 = (s32[8,128]{1,0:T(8,128)S(1)}, s32[8,128]{1,0:T(8,128)S(1)}, u32[]{:S(2)}, u32[]{:S(2)}) collective-permute-start(s32[8,128]{1,0:T(8,128)S(1)} %fusion), channel_id=1, source_target_pairs={{1,321},{3,323},{5,325},{7,327},{9,329},{11,331},{13,333},{15,335}... | collective-permute-start | bytes 12296 | tf_op jit(solution)/shard_map/ppermute | solution.py:421
  41.0 0.7 collective-permute-done.1
  41.7 119.0 %all_to_all.20 = bf16[64,176,128]{2,1,0:T(8,128)(2,1)S(1)} all-to-all(bf16[64,176,128]{2,1,0:T(8,128)(2,1)} %bitcast.19), channel_id=1, replica_groups=mesh['seq'=64,'head'=8] {'seq'}, dimensions={0} | all-to-all | bytes 5767168 | tf_op jit(solution)/shard_map/all_to_all | solution.py:396
  160.7 19.9 %dense_cluster_attention.1 = bf16[11264,128]{1,0:T(8,128)(2,1)} custom-call(bf16[11264,128]{1,0:T(8,128)(2,1)S(1)} %bitcast.16, s32[8,128]{1,0:T(8,128)S(1)} %max.7.refs_1_), custom_call_target="tpu_custom_call" | custom-call | tf_op jit(solution)/shard_map/dense_cluster_attention/pallas_call | solution.py:423
  180.7 0.0 copy-start
  180.7 7.6 %all-to-all-start.3 = ((bf16[64,176,128]{2,1,0:T(8,128)(2,1)}), bf16[64,176,128]{2,1,0:T(8,128)(2,1)S(1)}, u32[]{:S(2)}, u32[]{:S(2)}) async-start(bf16[64,176,128]{2,1,0:T(8,128)(2,1)} %bitcast.9), calls=%async_computation.3 | async-start | bytes 5767168 | tf_op jit(solution)/shard_map/all_to_all | solution.py:396
  188.3 104.5 %all-to-all-done.3 = bf16[64,176,128]{2,1,0:T(8,128)(2,1)S(1)} async-done(((bf16[64,176,128]{2,1,0:T(8,128)(2,1)}), bf16[64,176,128]{2,1,0:T(8,128)(2,1)S(1)}, u32[]{:S(2)}, u32[]{:S(2)}) %all-to-all-start.3) | async-done | bytes 2883616 | tf_op jit(solution)/shard_map/all_to_all | solution.py:396
  292.7 0.7 slice_reduce_fusion
  294.1 0.0 copy-done
  294.1 2.6 conditional.1
  294.1 2.6 dense_unpack_rows.1
  (4 shorter events, 0.0 us)
Async XLA Ops:
  6.8 19.5 %collective-permute-start = (s32[8,128]{1,0:T(8,128)S(1)}, s32[8,128]{1,0:T(8,128)S(1)}, u32[]{:S(2)}, u32[]{:S(2)}) collective-permute-start(s32[8,128]{1,0:T(8,128)S(1)} %slice_bitcast_fusion), channel_id=1, source_target_pairs={{1,321},{3,323},{5,325},{7,327},{9,329},{11,331},{13,333},{15,335}... | collective-permute-start | bytes 12296 | tf_op jit(solution)/shard_map/ppermute | solution.py:421
  26.3 15.5 %collective-permute-start.1 = (s32[8,128]{1,0:T(8,128)S(1)}, s32[8,128]{1,0:T(8,128)S(1)}, u32[]{:S(2)}, u32[]{:S(2)}) collective-permute-start(s32[8,128]{1,0:T(8,128)S(1)} %fusion), channel_id=1, source_target_pairs={{1,321},{3,323},{5,325},{7,327},{9,329},{11,331},{13,333},{15,335}... | collective-permute-start | bytes 12296 | tf_op jit(solution)/shard_map/ppermute | solution.py:421
  180.7 113.4 %copy-start = (s32[8,256,1]{1,2,0:T(1,128)S(1)}, s32[8,256,1]{1,2,0:T(1,128)}, u32[]{:S(2)}) copy-start(s32[8,256,1]{1,2,0:T(1,128)} %param.11) | copy-start | bytes 24580
  180.7 112.1 %all-to-all-start.3 = ((bf16[64,176,128]{2,1,0:T(8,128)(2,1)}), bf16[64,176,128]{2,1,0:T(8,128)(2,1)S(1)}, u32[]{:S(2)}, u32[]{:S(2)}) async-start(bf16[64,176,128]{2,1,0:T(8,128)(2,1)} %bitcast.9), calls=%async_computation.3 | async-start | bytes 5767168 | tf_op jit(solution)/shard_map/all_to_all | solution.py:396

commit v7 on v6

--- a/solution.py
+++ b/solution.py
@@ -16,7 +16,7 @@
 PACK_HEADS = 4
 ATTEND_HEADS = 2
 UNPACK_HEADS = 4
-TOKEN_HOPS = 2
+TOKEN_HOPS = 4
 
 
 def dot_nn(left, right):

time: 297 us -> 292 us (0.983)
  starting transfers between devices: 41 us -> 75.1 us
  waiting for transfers between devices: 106 us -> 75.7 us
  blocking collectives: 119 us -> 110 us
    all_to_all x1, waiting for transfers between devices: 104 us -> 71.7 us  [exchange(): lax.all_to_all(packed.reshape(owners, -1, packed.shape[1]), 'seq', split_...]
    ppermute x2 -> x4, starting transfers between devices: 33.4 us -> 64.6 us  [body(): token = jnp.maximum(token, lax.ppermute(token, ('seq', 'head'), turns))]
    all_to_all x1, blocking collectives: 119 us -> 110 us  [exchange(): lax.all_to_all(packed.reshape(owners, -1, packed.shape[1]), 'seq', split_...]
  transfers between devices with their start and end apart: 3 -> 5, of which waited for: 3 -> 5; matrix products, arithmetic and copies ran while one was open for 0% -> 0% of each run, Pallas kernels for 0% -> 0%
where the time goes in v7:
time: 292 us
  blocking collectives  110 us (38%)
  waiting for transfers between devices  75.7 us (26%)
  starting transfers between devices  75.1 us (26%)
  Pallas kernels  28.7 us (10%)
    all_to_all x1, blocking collectives, exchange(): lax.all_to_all(packed.reshape(owners, -1, packed.shape[1]), 'seq', split_...  110 us
    all_to_all x1, waiting for transfers between devices, exchange(): lax.all_to_all(packed.reshape(owners, -1, packed.shape[1]), 'seq', split_...  71.7 us
    ppermute x4, starting transfers between devices, body(): token = jnp.maximum(token, lax.ppermute(token, ('seq', 'head'), turns))  64.6 us
    pallas_call x1, Pallas kernels, body(): returned = exchange(attend(exchange(packed, owners), token), owners)  20 us
    all_to_all x1, starting transfers between devices, exchange(): lax.all_to_all(packed.reshape(owners, -1, packed.shape[1]), 'seq', split_...  10.4 us
    pallas_call x1, Pallas kernels, body(): packed, place = pack(routes, *tensors)  6.19 us
  transfers between devices with their start and end apart: 5, of which 5 were waited for; matrix products, arithmetic and copies ran while one was open for 0% of the time, Pallas kernels for 0%

profile of v7, /device:TPU:1, one launch (start us, length us, event | category | flops | bytes accessed | tf_op | source)
XLA Modules:
  0.0 291.7 jit_solution(13915587969488757030)
XLA Ops:
  0.6 6.2 %dense_pack_rows.1 = (bf16[11264,128]{1,0:T(8,128)(2,1)}, s32[8,1,256]{2,1,0:T(1,128)S(1)}) custom-call(s32[8,1,256]{2,1,0:T(1,128)} %bitcast.20, bf16[256,1024]{1,0:T(8,128)(2,1)} %refs_1_.1, bf16[256,1024]{1,0:T(8,128)(2,1)} %refs_2_.1, bf16[256,1024]{1,0:T(8,128)(2,1)} %refs_3_.1, bf16[256,1024]{1,0:T(8,128)(2,1)} %refs_4_.1), custom_call_target="tpu_custom_call" | custom-call | tf_op jit(solution)/shard_map/dense_pack_rows/pallas_call | solution.py:412
  6.8 18.7 %collective-permute-start = (s32[8,128]{1,0:T(8,128)S(1)}, s32[8,128]{1,0:T(8,128)S(1)}, u32[]{:S(2)}, u32[]{:S(2)}) collective-permute-start(s32[8,128]{1,0:T(8,128)S(1)} %slice_bitcast_fusion), channel_id=1, source_target_pairs={{1,321},{3,323},{5,325},{7,327},{9,329},{11,331},{13,333},{15,335}... | collective-permute-start | bytes 12296 | tf_op jit(solution)/shard_map/ppermute | solution.py:421
  25.6 0.7 collective-permute-done
  26.3 14.7 %collective-permute-start.1 = (s32[8,128]{1,0:T(8,128)S(1)}, s32[8,128]{1,0:T(8,128)S(1)}, u32[]{:S(2)}, u32[]{:S(2)}) collective-permute-start(s32[8,128]{1,0:T(8,128)S(1)} %fusion), channel_id=1, source_target_pairs={{1,321},{3,323},{5,325},{7,327},{9,329},{11,331},{13,333},{15,335}... | collective-permute-start | bytes 12296 | tf_op jit(solution)/shard_map/ppermute | solution.py:421
  41.0 0.7 collective-permute-done.1
  41.8 16.3 %collective-permute-start.2 = (s32[8,128]{1,0:T(8,128)S(1)}, s32[8,128]{1,0:T(8,128)S(1)}, u32[]{:S(2)}, u32[]{:S(2)}) collective-permute-start(s32[8,128]{1,0:T(8,128)S(1)} %max.13), channel_id=1, source_target_pairs={{1,321},{3,323},{5,325},{7,327},{9,329},{11,331},{13,333},{15,335}... | collective-permute-start | bytes 12296 | tf_op jit(solution)/shard_map/ppermute | solution.py:421
  58.1 1.8 collective-permute-done.2
  59.9 14.9 %collective-permute-start.3 = (s32[8,128]{1,0:T(8,128)S(1)}, s32[8,128]{1,0:T(8,128)S(1)}, u32[]{:S(2)}, u32[]{:S(2)}) collective-permute-start(s32[8,128]{1,0:T(8,128)S(1)} %max.14), channel_id=1, source_target_pairs={{1,321},{3,323},{5,325},{7,327},{9,329},{11,331},{13,333},{15,335}... | collective-permute-start | bytes 12296 | tf_op jit(solution)/shard_map/ppermute | solution.py:421
  74.8 0.7 collective-permute-done.3
  75.5 110.2 %all_to_all.20 = bf16[64,176,128]{2,1,0:T(8,128)(2,1)S(1)} all-to-all(bf16[64,176,128]{2,1,0:T(8,128)(2,1)} %bitcast.19), channel_id=1, replica_groups=mesh['seq'=64,'head'=8] {'seq'}, dimensions={0} | all-to-all | bytes 5767168 | tf_op jit(solution)/shard_map/all_to_all | solution.py:396
  185.7 20.0 %dense_cluster_attention.1 = bf16[11264,128]{1,0:T(8,128)(2,1)} custom-call(bf16[11264,128]{1,0:T(8,128)(2,1)S(1)} %bitcast.16, s32[8,128]{1,0:T(8,128)S(1)} %max.15.refs_1_), custom_call_target="tpu_custom_call" | custom-call | tf_op jit(solution)/shard_map/dense_cluster_attention/pallas_call | solution.py:423
  205.7 0.0 copy-start
  205.7 10.4 %all-to-all-start.3 = ((bf16[64,176,128]{2,1,0:T(8,128)(2,1)}), bf16[64,176,128]{2,1,0:T(8,128)(2,1)S(1)}, u32[]{:S(2)}, u32[]{:S(2)}) async-start(bf16[64,176,128]{2,1,0:T(8,128)(2,1)} %bitcast.9), calls=%async_computation.3 | async-start | bytes 5767168 | tf_op jit(solution)/shard_map/all_to_all | solution.py:396
  216.1 71.7 %all-to-all-done.3 = bf16[64,176,128]{2,1,0:T(8,128)(2,1)S(1)} async-done(((bf16[64,176,128]{2,1,0:T(8,128)(2,1)}), bf16[64,176,128]{2,1,0:T(8,128)(2,1)S(1)}, u32[]{:S(2)}, u32[]{:S(2)}) %all-to-all-start.3) | async-done | bytes 2883616 | tf_op jit(solution)/shard_map/all_to_all | solution.py:396
  287.8 0.7 slice_reduce_fusion
  289.1 0.0 copy-done
  289.1 2.6 conditional.1
  289.1 2.6 dense_unpack_rows.1
  (6 shorter events, 0.0 us)
Async XLA Ops:
  6.8 19.5 %collective-permute-start = (s32[8,128]{1,0:T(8,128)S(1)}, s32[8,128]{1,0:T(8,128)S(1)}, u32[]{:S(2)}, u32[]{:S(2)}) collective-permute-start(s32[8,128]{1,0:T(8,128)S(1)} %slice_bitcast_fusion), channel_id=1, source_target_pairs={{1,321},{3,323},{5,325},{7,327},{9,329},{11,331},{13,333},{15,335}... | collective-permute-start | bytes 12296 | tf_op jit(solution)/shard_map/ppermute | solution.py:421
  26.3 15.5 %collective-permute-start.1 = (s32[8,128]{1,0:T(8,128)S(1)}, s32[8,128]{1,0:T(8,128)S(1)}, u32[]{:S(2)}, u32[]{:S(2)}) collective-permute-start(s32[8,128]{1,0:T(8,128)S(1)} %fusion), channel_id=1, source_target_pairs={{1,321},{3,323},{5,325},{7,327},{9,329},{11,331},{13,333},{15,335}... | collective-permute-start | bytes 12296 | tf_op jit(solution)/shard_map/ppermute | solution.py:421
  41.8 18.1 %collective-permute-start.2 = (s32[8,128]{1,0:T(8,128)S(1)}, s32[8,128]{1,0:T(8,128)S(1)}, u32[]{:S(2)}, u32[]{:S(2)}) collective-permute-start(s32[8,128]{1,0:T(8,128)S(1)} %max.13), channel_id=1, source_target_pairs={{1,321},{3,323},{5,325},{7,327},{9,329},{11,331},{13,333},{15,335}... | collective-permute-start | bytes 12296 | tf_op jit(solution)/shard_map/ppermute | solution.py:421
  59.9 15.6 %collective-permute-start.3 = (s32[8,128]{1,0:T(8,128)S(1)}, s32[8,128]{1,0:T(8,128)S(1)}, u32[]{:S(2)}, u32[]{:S(2)}) collective-permute-start(s32[8,128]{1,0:T(8,128)S(1)} %max.14), channel_id=1, source_target_pairs={{1,321},{3,323},{5,325},{7,327},{9,329},{11,331},{13,333},{15,335}... | collective-permute-start | bytes 12296 | tf_op jit(solution)/shard_map/ppermute | solution.py:421
  205.7 83.4 %copy-start = (s32[8,256,1]{1,2,0:T(1,128)S(1)}, s32[8,256,1]{1,2,0:T(1,128)}, u32[]{:S(2)}) copy-start(s32[8,256,1]{1,2,0:T(1,128)} %param.11) | copy-start | bytes 24580
  205.7 82.1 %all-to-all-start.3 = ((bf16[64,176,128]{2,1,0:T(8,128)(2,1)}), bf16[64,176,128]{2,1,0:T(8,128)(2,1)S(1)}, u32[]{:S(2)}, u32[]{:S(2)}) async-start(bf16[64,176,128]{2,1,0:T(8,128)(2,1)} %bitcast.9), calls=%async_computation.3 | async-start | bytes 5767168 | tf_op jit(solution)/shard_map/all_to_all | solution.py:396
